TPU v7x, 32 devices: a whole 2x2x4 slice. The times are simulated.
32 devices in a mesh: groups: 2 (over y), out: 4 (over z), inp: 4 (over x, core).
Axes of the slice: x: 2, y: 2, z: 4, core: 2. Of those that a mesh axis runs over, the one named last changes fastest.
Arguments:
- acts_rot: bfloat16 [64, 8192], P(('groups', 'out', 'inp')), parts along dimension 0, may hold values from -6 to 6
- grads_rot: bfloat16 [64, 28672], P(('groups', 'out', 'inp')), parts along dimension 0, may hold values from -0.00024414062 to 0.00024414062
- query_grads: bfloat16 [8, 128, 28672], P('groups', None, 'out'), parts along dimension 0, may hold values from -6 to 6
- query_acts: bfloat16 [8, 128, 8192], P('groups', 'out', 'inp'), parts along dimension 0, may hold values from -0.5 to 0.5
- eigen: bfloat16 [28672, 8192], P('out', 'inp'), may hold values from 0.049804688 to 5
- block_mask: int32 [8, 224, 64], P('groups'), parts along dimension 0, may hold values from 0 to 1, as said below
- order: int32 [64], P('groups'), parts along dimension 0, may hold values from 0 to 31, each once
- segment_ids: int32 [64], P('groups'), parts along dimension 0, may hold values from 0 to 3, never falling along the last dimension, each value on 1 to 16 neighbouring positions
Outputs:
- token_scores: float32 [4, 64], P(None, 'groups'), parts along dimension 1
- seq_scores: float32 [8, 4], P('groups'), parts along dimension 0
There are 2 independent parts, one for each index of `groups`. A program takes and returns all parts, laid end to end along the dimension named above; an argument that names none is the same for every part. Nothing has to cross between parts.
Inputs may be any that keep to these rules, and one draw needn't show every extreme that they name: block_mask[q, r, c] is 1 where query q keeps the block of rows r * 128 to r * 128 + 127 and columns c * 128 to c * 128 + 127, else 0. order holds each of the 32 positions once. segment_ids never falls along the positions; each sequence has 1 to 16 positions and one has exactly 16.
All inputs are finite; a program needn't handle non-finite values.
Results may differ from a plain program's by a relative error of at most 0.0035.
Values may be sent and summed in bfloat16 or wider, within the bound.
No kernel may reach another device: no remote copies, remote signals or barrier semaphores. Data moves between devices by JAX's collectives and lax.ppermute only.
A program may use at most 512 MiB of HBM per device.

v0:
```python
import functools
import math

import jax
import jax.numpy as jnp
from jax import lax
from jax.experimental import pallas as pl
from jax.experimental.pallas import tpu as pltpu
from jax.sharding import PartitionSpec as P


BLOCK = 128
SEQS = 4
UNROLL = 16
CHUNKS = 2
FLIGHT = 4
SLOT_BITS = 10

damping = 0.1


def score_kernel(
    unit, piece, first_col, shard_count, has_base,
    place_ref, end_ref, packed_ref,
    eigen_hbm, queries_hbm, near_ref, map_ref, *rest,
):
    if has_base:
        base_ref, rest = rest[0], rest[1:]
    shards, rest = rest[:shard_count], rest[shard_count:]
    out_ref, eigen_ref, queries_ref, weights_ref, grads_scr, sums_ref, sems = rest[:7]
    hold_a, hold_b = rest[7:][: UNROLL // 2], rest[7:][UNROLL // 2 :]
    rows, width = eigen_ref.shape
    queries = queries_hbm.shape[0]
    col_blocks = width // BLOCK
    pieces = rows // piece

    def copies(p):
        at = pl.ds(pl.multiple_of(p * piece, piece), piece)
        part = (slice(None), slice(None), at)
        if unit < BLOCK:
            part = (slice(None), pl.ds(p * (piece // unit), piece // unit))
        return (
            pltpu.make_async_copy(
                eigen_hbm.at[at, pl.ds(first_col, width)], eigen_ref.at[at, :], sems.at[0, p]
            ),
            pltpu.make_async_copy(queries_hbm.at[part], queries_ref.at[part], sems.at[1, p]),
        )

    for p in range(min(FLIGHT, pieces)):
        for copy in copies(p):
            copy.start()

    sums_ref[...] = jnp.zeros_like(sums_ref)
    weights_ref[queries * col_blocks] = jnp.zeros(weights_ref.shape[1:], weights_ref.dtype)
    for k, shard in enumerate(shards):
        held = shard.shape[1]
        place = pl.multiple_of(place_ref[k] * held, held)
        for q in range(queries):
            for c in range(col_blocks):
                weights_ref[q * col_blocks + c, pl.ds(place, held), :] = shard[
                    q, :, c * BLOCK : (c + 1) * BLOCK
                ]
    for r in range(rows // unit):
        grads_scr[r] = near_ref[:, r * unit : (r + 1) * unit]
    for h in hold_b:
        h[...] = jnp.zeros_like(h)

    half = UNROLL // 2

    def entry(at):
        code = packed_ref[at]
        low = (1 << SLOT_BITS) - 1
        return code >> 2 * SLOT_BITS, code >> SLOT_BITS & low, code & low

    def outer_to(at, hold):
        row, slot_a, slot_b = entry(at)
        query = jnp.minimum(lax.div(slot_a, col_blocks), queries - 1)
        rows_at = pl.ds(pl.multiple_of(row * unit, unit), unit)
        right = jnp.concatenate([weights_ref[slot_a], weights_ref[slot_b]], axis=1)
        left = queries_ref[query, :, rows_at] if unit == BLOCK else queries_ref[query, row]
        outer = lax.dot_general(
            left, right, (((0,), (0,)), ((), ())), preferred_element_type=jnp.float32
        )
        for h, slot in enumerate((slot_a, slot_b)):
            cols = pl.ds(pl.multiple_of(lax.rem(slot, col_blocks) * BLOCK, BLOCK), BLOCK)
            scale = 1.0 / (eigen_ref[rows_at, cols].astype(jnp.float32) + damping)
            hold[:, h * BLOCK : (h + 1) * BLOCK] = (
                outer[:, h * BLOCK : (h + 1) * BLOCK] * scale
            ).astype(jnp.bfloat16)

    def add_part(at, hold):
        row, slot_a, slot_b = entry(at)
        part = jnp.dot(grads_scr[row], hold[...], preferred_element_type=jnp.float32)
        sums_ref[slot_a] += part[:, :BLOCK]
        sums_ref[slot_b] += part[:, BLOCK:]

    def batch(k, before):
        start = k * UNROLL
        for s1, s2, at1, at2 in ((hold_a, hold_b, start, before), (hold_b, hold_a, start + half, start)):
            for u in range(half):
                outer_to(at1 + u, s1[u])
                add_part(at2 + u, s2[u])
        return start + half

    def one_piece(p, carry):
        k, before = carry
        for copy in copies(p):
            copy.wait()

        @pl.when(p + FLIGHT < pieces)
        def _():
            for copy in copies(p + FLIGHT):
                copy.start()

        end = end_ref[p]
        return end, lax.fori_loop(k, end, batch, before)

    idle = packed_ref.shape[0] - UNROLL
    _, before = lax.fori_loop(0, pieces, one_piece, (jnp.int32(0), jnp.int32(idle)))
    for u in range(half):
        add_part(before + u, hold_b[u])

    for q in range(queries):
        total = jnp.zeros(sums_ref.shape[1:], jnp.float32)
        for c in range(col_blocks):
            at = rows + first_col + c * BLOCK
            total += sums_ref[q * col_blocks + c] * near_ref[:, at : at + BLOCK].astype(jnp.float32)
        score = jnp.sum(total, axis=1, keepdims=True)
        mapped = jnp.sum(score * map_ref[...], axis=0, keepdims=True)
        out_ref[q : q + 1, :] = base_ref[q : q + 1, :] + mapped if has_base else mapped


def block_lists(mask, unit, piece, chunks):
    queries, row_units, _ = mask.shape
    mask = mask.reshape(queries, row_units, chunks, -1).transpose(2, 1, 0, 3)
    col_blocks = mask.shape[3]
    half = (col_blocks + 1) // 2
    kept = mask.astype(jnp.int32)
    col = jnp.arange(col_blocks, dtype=jnp.int32)
    rank = jnp.sum(jnp.where(col[None, :] < col[:, None], kept[..., None, :], 0), axis=-1)
    pair = jnp.arange(half, dtype=jnp.int32)
    hit = jnp.where(mask, rank, -1)[..., None, :]
    col_a = jnp.sum(jnp.where(hit == 2 * pair[:, None], col, 0), axis=-1)
    col_b = jnp.sum(jnp.where(hit == 2 * pair[:, None] + 1, col, 0), axis=-1)
    count = jnp.sum(kept, axis=-1)[..., None]
    has_a, has_b = count > 2 * pair, count > 2 * pair + 1
    row = jnp.arange(row_units, dtype=jnp.int32)[:, None, None]
    query = jnp.arange(queries, dtype=jnp.int32)[:, None]
    spare = queries * col_blocks
    slot_a = query * col_blocks + col_a
    slot_b = jnp.where(has_b, query * col_blocks + col_b, spare)
    code = ((row << SLOT_BITS | slot_a) << SLOT_BITS | slot_b) + 1
    code = jnp.where(has_a, code, 0).reshape(chunks, -1)
    entries = code.shape[1]
    length = -(-entries // UNROLL) * UNROLL + UNROLL
    at = jnp.arange(entries, dtype=jnp.int32)
    place = jnp.sum(((at[None, :] < at[:, None]) & (code > 0)[:, None, :]).astype(jnp.int32), axis=2)
    place = jnp.where(code > 0, place, -1)
    slots = jnp.arange(length, dtype=jnp.int32)
    packed = jnp.sum(jnp.where(place[:, None, :] == slots[:, None], code[:, None, :], 0), axis=2)
    packed = jnp.where(packed > 0, packed - 1, spare << SLOT_BITS | spare)
    pieces = row_units * unit // piece
    begin = jnp.arange(pieces, dtype=jnp.int32) * (entries // pieces)
    upto = jnp.sum(
        ((at[None, :] < begin[:, None] + entries // pieces) & (code > 0)[:, None, :]).astype(jnp.int32), axis=2
    )
    last = jnp.arange(pieces) == pieces - 1
    ends = jnp.where(last, -(-upto // UNROLL), upto // UNROLL).astype(jnp.int32)
    return ends, packed


def score_part(lists, eigen, query_grads, shards, places, near, mapping, base, unit, piece, first_col, width):
    queries = query_grads.shape[0]
    rows = eigen.shape[0]
    query_tokens = shards[0].shape[1] * len(shards)
    tokens = near.shape[0]
    col_blocks = width // BLOCK
    kernel = functools.partial(score_kernel, unit, piece, first_col, len(shards), base is not None)
    extra = [] if base is None else [base]
    vmem, hbm = pl.BlockSpec(memory_space=pltpu.VMEM), pl.BlockSpec(memory_space=pl.ANY)
    return pl.pallas_call(
        kernel,
        in_specs=[pl.BlockSpec(memory_space=pltpu.SMEM)] * 3 + [hbm, hbm] + [vmem] * (2 + len(extra) + len(shards)),
        out_specs=vmem,
        scratch_shapes=[
            pltpu.VMEM((rows, width), jnp.bfloat16),
            pltpu.VMEM(query_grads.shape, jnp.bfloat16),
            pltpu.VMEM((queries * col_blocks + 1, query_tokens, BLOCK), jnp.bfloat16),
            pltpu.VMEM((rows // unit, tokens, unit), jnp.bfloat16),
            pltpu.VMEM((queries * col_blocks + 1, tokens, BLOCK), jnp.float32),
            pltpu.SemaphoreType.DMA((2, rows // piece)),
            *[pltpu.VMEM((unit, 2 * BLOCK), jnp.bfloat16)] * UNROLL,
        ],
        out_shape=jax.ShapeDtypeStruct((queries, mapping.shape[1]), jnp.float32),
        compiler_params=pltpu.CompilerParams(vmem_limit_bytes=56 << 20),
    )(places, *lists, eigen, query_grads, near, mapping, *extra, *shards)


def is_small_power(n):
    return n in (1, 2, 4)


def exchange(make, axis, n):
    got = [make(0)]
    for k in range(1, n):
        payload = make(k)
        got.append(lax.ppermute(payload, axis, [(s, s ^ k) for s in range(n)]))
    return got


def scores_of(n_out, n_inp, acts_rot, grads_rot, query_grads, query_acts, eigen, block_mask, order, segment_ids):
    rows, cols = eigen.shape
    queries = block_mask.shape[0]
    held = acts_rot.shape[0]
    tokens = order.shape[0]
    at_out, at_inp = lax.axis_index("out"), lax.axis_index("inp")
    unit = math.gcd(rows, BLOCK)
    tile = max(t for t in range(unit, 512 + 1, unit) if rows % t == 0 and (t % BLOCK == 0 or t == rows))
    chunks = CHUNKS if (cols // BLOCK) % CHUNKS == 0 else 1
    width = cols // chunks
    row_units = rows // unit
    direct = is_small_power(n_out) and is_small_power(n_inp)
    t = jnp.arange(tokens, dtype=jnp.int32)

    if direct:
        near = exchange(
            lambda k: jnp.concatenate(
                [lax.dynamic_slice_in_dim(grads_rot, (at_out ^ k) * rows, rows, 1), acts_rot], axis=1
            ),
            "out", n_out,
        )
        shards = [
            exchange(lambda k: query_acts[:, :, c * width : (c + 1) * width], "out", n_out)
            for c in range(chunks)
        ]
        places = at_out ^ jnp.arange(n_out, dtype=jnp.int32)
    else:
        spread = lax.all_to_all(grads_rot[None], "out", split_axis=2, concat_axis=0, tiled=True)
        grads = lax.all_gather(spread, "inp", axis=1, tiled=True).reshape(-1, rows)
        whole_acts = lax.all_gather(acts_rot, ("out", "inp"), axis=0, tiled=True)
        acts = lax.dynamic_slice_in_dim(whole_acts, at_inp * cols, cols, 1)
        near = jnp.concatenate([grads, acts], axis=1)
        whole = lax.all_gather(query_acts, "out", axis=1, tiled=True)
        shards = [[whole[:, :, c * width : (c + 1) * width]] for c in range(chunks)]
        places = jnp.zeros((1,), jnp.int32)

    if unit < BLOCK:
        query_grads = query_grads.reshape(queries, -1, row_units, unit).transpose(0, 2, 1, 3)

    row_at = at_out * rows
    if rows % BLOCK == 0:
        band = lax.dynamic_slice_in_dim(block_mask, row_at // BLOCK, row_units, 1)
    else:
        band = jnp.take(block_mask, (row_at + unit * jnp.arange(row_units)) // BLOCK, axis=1)
    band = lax.dynamic_slice_in_dim(band, at_inp * (cols // BLOCK), cols // BLOCK, 2) > 0
    ends, packed = block_lists(band, unit, tile, chunks)

    if direct:
        near = jnp.concatenate(near, axis=0)
        both = exchange(
            lambda k: jnp.concatenate(
                [near[:, :rows], lax.dynamic_slice_in_dim(near, rows + (at_inp ^ k) * cols, cols, 1)],
                axis=1,
            ),
            "inp", n_inp,
        )
        near = jnp.concatenate(both, axis=0)
        per_inp = held * n_out
        from_inp = at_inp ^ (t // per_inp)
        from_out = at_out ^ (t % per_inp // held)
        arrived = (from_out * n_inp + from_inp) * held + t % held
    else:
        arrived = t
    position = jnp.sum(jnp.where(arrived[:, None] == t[None, :], order[None, :], 0), axis=1)
    sequence = jnp.sum(jnp.where(position[:, None] == t[None, :], segment_ids[None, :], 0), axis=1)
    reach = -(-(tokens + SEQS) // BLOCK) * BLOCK
    column = jnp.arange(reach, dtype=jnp.int32)[None, :]
    mapping = (
        (column == position[:, None]) | (column == tokens + sequence[:, None])
    ).astype(jnp.float32)

    scores = None
    for c in range(chunks):
        scores = score_part(
            (ends[c], packed[c]), eigen, query_grads, shards[c], places, near, mapping, scores,
            unit, tile, c * width, width,
        )
    if direct:
        for axis, n in (("inp", n_inp), ("out", n_out)):
            k = 1
            while k < n:
                scores = scores + lax.ppermute(scores, axis, [(s, s ^ k) for s in range(n)])
                k *= 2
    else:
        scores = lax.psum(scores, ("out", "inp"))
    return scores[:, :tokens], scores[:, tokens : tokens + SEQS]


def solution(mesh):
    in_specs = (
        P(("groups", "out", "inp"), None),
        P(("groups", "out", "inp"), None),
        P("groups", None, "out"),
        P("groups", "out", "inp"),
        P("out", "inp"),
        P("groups", None, None),
        P("groups"),
        P("groups"),
    )
    out_specs = (P(None, "groups"), P("groups", None))
    return jax.shard_map(
        functools.partial(scores_of, mesh.shape["out"], mesh.shape["inp"]),
        mesh=mesh, in_specs=in_specs, out_specs=out_specs, check_vma=False,
    )
```

profile of v0, /device:TPU:0, one launch (start us, length us, event | category | flops | bytes accessed | tf_op | source)
XLA Modules:
  0.0 105.8 jit_solution(7644147270289328146)
XLA Ops:
  0.6 1.1 %fusion.17 = (bf16[4,32,1024]{2,1,0:T(8,128)(2,1)S(1)}, bf16[4,32,1024]{2,1,0:T(8,128)(2,1)S(1)}) fusion(bf16[4,32,2048]{2,1,0:T(8,128)(2,1)} %param.11), kind=kLoop, calls=%fused_computation.87 | loop fusion | bytes 1048576 | tf_op jit(solution)/shard_map/slice | solution.py:233
  1.7 3.1 %collective-permute-start.6 = (bf16[4,32,1024]{2,1,0:T(8,128)(2,1)S(1)}, bf16[4,32,1024]{2,1,0:T(8,128)(2,1)S(1)}, u32[]{:S(2)}, u32[]{:S(2)}) collective-permute-start(bf16[4,32,1024]{2,1,0:T(8,128)(2,1)S(1)} %get-tuple-element.9.rest_0_), channel_id=1, source_target_pairs={{0,4},{4,0},{8,12},{12,8},{1,5},{5,1},{9,13},{13,9},{2,6},{6,2},{1... | collective-permute-start | bytes 786440 | tf_op jit(solution)/shard_map/ppermute | solution.py:207
  4.8 2.6 %collective-permute-start.7 = (bf16[4,32,1024]{2,1,0:T(8,128)(2,1)S(1)}, bf16[4,32,1024]{2,1,0:T(8,128)(2,1)S(1)}, u32[]{:S(2)}, u32[]{:S(2)}) collective-permute-start(bf16[4,32,1024]{2,1,0:T(8,128)(2,1)S(1)} %get-tuple-element.9.rest_0_), channel_id=1, source_target_pairs={{0,8},{4,12},{8,0},{12,4},{1,9},{5,13},{9,1},{13,5},{2,10},{6,14},... | collective-permute-start | bytes 786440 | tf_op jit(solution)/shard_map/ppermute | solution.py:207
  7.4 0.9 constant_dynamic-slice_fusion.7
  8.3 0.9 pad_maximum_fusion.5
  9.3 1.9 %collective-permute-start.1 = (bf16[2,15360]{1,0:T(2,128)(2,1)S(1)}, bf16[2,15360]{1,0:T(2,128)(2,1)S(1)}, u32[]{:S(2)}, u32[]{:S(2)}) collective-permute-start(bf16[2,15360]{1,0:T(2,128)(2,1)S(1)} %get-tuple-element.22), channel_id=1, source_target_pairs={{0,8},{4,12},{8,0},{12,4},{1,9},{5,13},{9,1},{13,5},{2,10},{6,14},... | collective-permute-start | bytes 184328 | tf_op jit(solution)/shard_map/ppermute | solution.py:207
  11.2 2.5 %collective-permute-start = (bf16[2,15360]{1,0:T(2,128)(2,1)S(1)}, bf16[2,15360]{1,0:T(2,128)(2,1)S(1)}, u32[]{:S(2)}, u32[]{:S(2)}) collective-permute-start(bf16[2,15360]{1,0:T(2,128)(2,1)S(1)} %get-tuple-element.21), channel_id=1, source_target_pairs={{0,4},{4,0},{8,12},{12,8},{1,5},{5,1},{9,13},{13,9},{2,6},{6,2},{1... | collective-permute-start | bytes 184328 | tf_op jit(solution)/shard_map/ppermute | solution.py:207
  13.7 0.2 iota_compare_fusion.1
  14.0 1.0 bitcast_convert_fusion
  15.1 1.0 fusion.4
  16.5 0.2 reduce_sum.90
  16.9 0.2 gt.82
  17.1 0.3 gt.83
  17.7 0.2 reduce_sum.88
  18.7 0.3 fusion
  19.0 0.8 convert_reduce_fusion
  19.8 0.8 select_reduce_fusion
  20.7 0.2 select_reduce_fusion.5
  20.9 0.2 select_reduce_fusion.4
  21.0 0.7 fusion.3.map_ref
  21.8 0.6 fusion.18
  22.4 2.0 %collective-permute-done.1 = bf16[2,15360]{1,0:T(2,128)(2,1)S(1)} collective-permute-done((bf16[2,15360]{1,0:T(2,128)(2,1)S(1)}, bf16[2,15360]{1,0:T(2,128)(2,1)S(1)}, u32[]{:S(2)}, u32[]{:S(2)}) %collective-permute-start.1) | collective-permute-done | bytes 61472 | tf_op jit(solution)/shard_map/ppermute | solution.py:207
  24.4 0.3 pad_maximum_fusion.1
  24.9 1.6 %collective-permute-start.4 = (bf16[8,9216]{1,0:T(8,128)(2,1)S(1)}, bf16[8,9216]{1,0:T(8,128)(2,1)S(1)}, u32[]{:S(2)}, u32[]{:S(2)}) collective-permute-start(bf16[8,9216]{1,0:T(8,128)(2,1)S(1)} %get-tuple-element.15), channel_id=1, source_target_pairs={{0,2},{1,3},{2,0},{3,1},{4,6},{5,7},{6,4},{7,5},{8,10},{9,11},{10,... | collective-permute-start | bytes 442376 | tf_op jit(solution)/shard_map/ppermute | solution.py:207
  26.5 0.3 collective-permute-start.3
  26.7 0.6 iota_xor_fusion.place_ref
  27.3 0.7 slice_reduce_fusion
  28.0 3.0 %collective-permute-done.5 = bf16[8,9216]{1,0:T(8,128)(2,1)S(1)} collective-permute-done((bf16[8,9216]{1,0:T(8,128)(2,1)S(1)}, bf16[8,9216]{1,0:T(8,128)(2,1)S(1)}, u32[]{:S(2)}, u32[]{:S(2)}) %collective-permute-start.5) | collective-permute-done | bytes 147488 | tf_op jit(solution)/shard_map/ppermute | solution.py:207
  31.0 2.5 %collective-permute-start.8 = (bf16[4,32,1024]{2,1,0:T(8,128)(2,1)S(1)}, bf16[4,32,1024]{2,1,0:T(8,128)(2,1)S(1)}, u32[]{:S(2)}, u32[]{:S(2)}) collective-permute-start(bf16[4,32,1024]{2,1,0:T(8,128)(2,1)S(1)} %get-tuple-element.9.rest_0_), channel_id=1, source_target_pairs={{0,12},{4,8},{8,4},{12,0},{1,13},{5,9},{9,5},{13,1},{2,14},{6,10},... | collective-permute-start | bytes 786440 | tf_op jit(solution)/shard_map/ppermute | solution.py:207
  33.5 0.7 collective-permute-done.4
  34.2 3.0 %collective-permute-start.10 = (bf16[4,32,1024]{2,1,0:T(8,128)(2,1)S(1)}, bf16[4,32,1024]{2,1,0:T(8,128)(2,1)S(1)}, u32[]{:S(2)}, u32[]{:S(2)}) collective-permute-start(bf16[4,32,1024]{2,1,0:T(8,128)(2,1)S(1)} %get-tuple-element.8.rest_1_), channel_id=1, source_target_pairs={{0,8},{4,12},{8,0},{12,4},{1,9},{5,13},{9,1},{13,5},{2,10},{6,14},... | collective-permute-start | bytes 786440 | tf_op jit(solution)/shard_map/ppermute | solution.py:207
  37.2 1.4 %collective-permute-start.11 = (bf16[4,32,1024]{2,1,0:T(8,128)(2,1)S(1)}, bf16[4,32,1024]{2,1,0:T(8,128)(2,1)S(1)}, u32[]{:S(2)}, u32[]{:S(2)}) collective-permute-start(bf16[4,32,1024]{2,1,0:T(8,128)(2,1)S(1)} %get-tuple-element.8.rest_1_), channel_id=1, source_target_pairs={{0,12},{4,8},{8,4},{12,0},{1,13},{5,9},{9,5},{13,1},{2,14},{6,10},... | collective-permute-start | bytes 786440 | tf_op jit(solution)/shard_map/ppermute | solution.py:207
  38.7 0.9 pad_maximum_fusion.near_ref
  39.5 2.5 %collective-permute-done.8.rest_3_ = bf16[4,32,1024]{2,1,0:T(8,128)(2,1)S(1)} collective-permute-done((bf16[4,32,1024]{2,1,0:T(8,128)(2,1)S(1)}, bf16[4,32,1024]{2,1,0:T(8,128)(2,1)S(1)}, u32[]{:S(2)}, u32[]{:S(2)}) %collective-permute-start.8) | collective-permute-done | bytes 262176 | tf_op jit(solution)/shard_map/ppermute | solution.py:207
  42.1 0.7 copy-done.6
  42.8 16.6 %shard_map.95.rest_0_ = f32[4,128]{1,0:T(4,128)} custom-call(s32[4]{0:T(128)} %iota_xor_fusion.place_ref, s32[14]{0:T(128)} %get-tuple-element.4.end_ref, s32[912]{0:T(1024)} %bitcast.13, bf16[7168,2048]{1,0:T(8,128)(2,1)} %eigen_hbm.3, bf16[4,128,7168]{2,1,0:T(8,128)(2,1)} %queries_hbm.3, bf16[32,9216]{1,0:T(8,128)(2,1)} %pad_maximum_fusion.near_ref, ...), custom_call_target="tpu_custom_call" | custom-call | tf_op jit(solution)/shard_map/pallas_call | solution.py:181
  59.3 2.6 %collective-permute-done.10.rest_3_ = bf16[4,32,1024]{2,1,0:T(8,128)(2,1)S(1)} collective-permute-done((bf16[4,32,1024]{2,1,0:T(8,128)(2,1)S(1)}, bf16[4,32,1024]{2,1,0:T(8,128)(2,1)S(1)}, u32[]{:S(2)}, u32[]{:S(2)}) %collective-permute-start.10) | collective-permute-done | bytes 262176 | tf_op jit(solution)/shard_map/ppermute | solution.py:207
  62.0 0.7 copy-done.5
  62.8 16.7 %shard_map.96 = f32[4,128]{1,0:T(4,128)} custom-call(s32[4]{0:T(128)} %iota_xor_fusion.place_ref, s32[14]{0:T(128)} %get-tuple-element.5.end_ref, s32[912]{0:T(1024)} %bitcast.12, bf16[7168,2048]{1,0:T(8,128)(2,1)} %eigen_hbm.3, bf16[4,128,7168]{2,1,0:T(8,128)(2,1)} %queries_hbm.3, bf16[32,9216]{1,0:T(8,128)(2,1)} %pad_maximum_fusion.near_ref, ...), custom_call_target="tpu_custom_call" | custom-call | tf_op jit(solution)/shard_map/pallas_call | solution.py:181
  79.6 1.4 %collective-permute-done.12 = f32[4,128]{1,0:T(4,128)S(1)} collective-permute-done((f32[4,128]{1,0:T(4,128)}, f32[4,128]{1,0:T(4,128)S(1)}, u32[]{:S(2)}, u32[]{:S(2)}) %collective-permute-start.12) | collective-permute-done | bytes 2080 | tf_op jit(solution)/shard_map/ppermute | solution.py:292
  80.9 0.7 add.238
  81.6 1.4 %collective-permute-start.13 = (f32[4,128]{1,0:T(4,128)S(1)}, f32[4,128]{1,0:T(4,128)S(1)}, u32[]{:S(2)}, u32[]{:S(2)}) collective-permute-start(f32[4,128]{1,0:T(4,128)S(1)} %add.238), channel_id=1, source_target_pairs={{0,2},{1,3},{2,0},{3,1},{4,6},{5,7},{6,4},{7,5},{8,10},{9,11},{10,... | collective-permute-start | bytes 6152 | tf_op jit(solution)/shard_map/ppermute | solution.py:292
  83.0 2.2 %collective-permute-done.13 = f32[4,128]{1,0:T(4,128)S(1)} collective-permute-done((f32[4,128]{1,0:T(4,128)S(1)}, f32[4,128]{1,0:T(4,128)S(1)}, u32[]{:S(2)}, u32[]{:S(2)}) %collective-permute-start.13) | collective-permute-done | bytes 2080 | tf_op jit(solution)/shard_map/ppermute | solution.py:292
  85.2 13.8 %collective-permute-start.14 = (f32[4,128]{1,0:T(4,128)S(1)}, f32[4,128]{1,0:T(4,128)S(1)}, u32[]{:S(2)}, u32[]{:S(2)}) collective-permute-start(f32[4,128]{1,0:T(4,128)S(1)} %add.239), channel_id=1, source_target_pairs={{0,4},{4,0},{8,12},{12,8},{1,5},{5,1},{9,13},{13,9},{2,6},{6,2},{1... | collective-permute-start | bytes 6152 | tf_op jit(solution)/shard_map/ppermute | solution.py:292
  99.0 1.6 %collective-permute-done.14 = f32[4,128]{1,0:T(4,128)S(1)} collective-permute-done((f32[4,128]{1,0:T(4,128)S(1)}, f32[4,128]{1,0:T(4,128)S(1)}, u32[]{:S(2)}, u32[]{:S(2)}) %collective-permute-start.14) | collective-permute-done | bytes 2080 | tf_op jit(solution)/shard_map/ppermute | solution.py:292
  100.6 3.1 %collective-permute-start.15 = (f32[4,128]{1,0:T(4,128)S(1)}, f32[4,128]{1,0:T(4,128)S(1)}, u32[]{:S(2)}, u32[]{:S(2)}) collective-permute-start(f32[4,128]{1,0:T(4,128)S(1)} %add.240), channel_id=1, source_target_pairs={{0,8},{4,12},{8,0},{12,4},{1,9},{5,13},{9,1},{13,5},{2,10},{6,14},... | collective-permute-start | bytes 6152 | tf_op jit(solution)/shard_map/ppermute | solution.py:292
  103.6 1.6 %collective-permute-done.15 = f32[4,128]{1,0:T(4,128)S(1)} collective-permute-done((f32[4,128]{1,0:T(4,128)S(1)}, f32[4,128]{1,0:T(4,128)S(1)}, u32[]{:S(2)}, u32[]{:S(2)}) %collective-permute-start.15) | collective-permute-done | bytes 2080 | tf_op jit(solution)/shard_map/ppermute | solution.py:292
  105.2 0.6 slice.44
  (65 shorter events, 2.3 us)
Async XLA Ops:
  1.7 29.3 %copy-start.1 = (bf16[4,32,1024]{2,1,0:T(8,128)(2,1)}, bf16[4,32,1024]{2,1,0:T(8,128)(2,1)S(1)}, u32[]{:S(2)}) copy-start(bf16[4,32,1024]{2,1,0:T(8,128)(2,1)S(1)} %get-tuple-element.9.rest_0_) | copy-start | bytes 786436
  1.7 35.5 %copy-start = (bf16[4,32,1024]{2,1,0:T(8,128)(2,1)}, bf16[4,32,1024]{2,1,0:T(8,128)(2,1)S(1)}, u32[]{:S(2)}) copy-start(bf16[4,32,1024]{2,1,0:T(8,128)(2,1)S(1)} %get-tuple-element.8.rest_1_) | copy-start | bytes 786436
  1.7 35.5 %collective-permute-start.6 = (bf16[4,32,1024]{2,1,0:T(8,128)(2,1)S(1)}, bf16[4,32,1024]{2,1,0:T(8,128)(2,1)S(1)}, u32[]{:S(2)}, u32[]{:S(2)}) collective-permute-start(bf16[4,32,1024]{2,1,0:T(8,128)(2,1)S(1)} %get-tuple-element.9.rest_0_), channel_id=1, source_target_pairs={{0,4},{4,0},{8,12},{12,8},{1,5},{5,1},{9,13},{13,9},{2,6},{6,2},{1... | collective-permute-start | bytes 786440 | tf_op jit(solution)/shard_map/ppermute | solution.py:207
  4.8 34.7 %collective-permute-start.7 = (bf16[4,32,1024]{2,1,0:T(8,128)(2,1)S(1)}, bf16[4,32,1024]{2,1,0:T(8,128)(2,1)S(1)}, u32[]{:S(2)}, u32[]{:S(2)}) collective-permute-start(bf16[4,32,1024]{2,1,0:T(8,128)(2,1)S(1)} %get-tuple-element.9.rest_0_), channel_id=1, source_target_pairs={{0,8},{4,12},{8,0},{12,4},{1,9},{5,13},{9,1},{13,5},{2,10},{6,14},... | collective-permute-start | bytes 786440 | tf_op jit(solution)/shard_map/ppermute | solution.py:207
  9.2 13.2 %collective-permute-start.2 = (bf16[2,15360]{1,0:T(2,128)(2,1)S(1)}, bf16[2,15360]{1,0:T(2,128)(2,1)S(1)}, u32[]{:S(2)}, u32[]{:S(2)}) collective-permute-start(bf16[2,15360]{1,0:T(2,128)(2,1)S(1)} %get-tuple-element.23), channel_id=1, source_target_pairs={{0,12},{4,8},{8,4},{12,0},{1,13},{5,9},{9,5},{13,1},{2,14},{6,10},... | collective-permute-start | bytes 184328 | tf_op jit(solution)/shard_map/ppermute | solution.py:207
  9.3 15.2 %collective-permute-start.1 = (bf16[2,15360]{1,0:T(2,128)(2,1)S(1)}, bf16[2,15360]{1,0:T(2,128)(2,1)S(1)}, u32[]{:S(2)}, u32[]{:S(2)}) collective-permute-start(bf16[2,15360]{1,0:T(2,128)(2,1)S(1)} %get-tuple-element.22), channel_id=1, source_target_pairs={{0,8},{4,12},{8,0},{12,4},{1,9},{5,13},{9,1},{13,5},{2,10},{6,14},... | collective-permute-start | bytes 184328 | tf_op jit(solution)/shard_map/ppermute | solution.py:207
  11.2 13.3 %collective-permute-start = (bf16[2,15360]{1,0:T(2,128)(2,1)S(1)}, bf16[2,15360]{1,0:T(2,128)(2,1)S(1)}, u32[]{:S(2)}, u32[]{:S(2)}) collective-permute-start(bf16[2,15360]{1,0:T(2,128)(2,1)S(1)} %get-tuple-element.21), channel_id=1, source_target_pairs={{0,4},{4,0},{8,12},{12,8},{1,5},{5,1},{9,13},{13,9},{2,6},{6,2},{1... | collective-permute-start | bytes 184328 | tf_op jit(solution)/shard_map/ppermute | solution.py:207
  16.5 4.2 %copy-start.10 = (s32[32]{0:T(128)S(1)}, s32[32]{0:T(128)}, u32[]{:S(2)}) copy-start(s32[32]{0:T(128)} %param.14) | copy-start | bytes 388
  16.5 4.4 %copy-start.11 = (s32[32]{0:T(128)S(1)}, s32[32]{0:T(128)}, u32[]{:S(2)}) copy-start(s32[32]{0:T(128)} %param.15) | copy-start | bytes 388
  16.5 7.9 %copy-start.8 = (bf16[2,8192]{1,0:T(2,128)(2,1)S(1)}, bf16[2,8192]{1,0:T(2,128)(2,1)}, u32[]{:S(2)}) copy-start(bf16[2,8192]{1,0:T(2,128)(2,1)} %param.8) | copy-start | bytes 98308
  24.8 6.2 %collective-permute-start.5 = (bf16[8,9216]{1,0:T(8,128)(2,1)S(1)}, bf16[8,9216]{1,0:T(8,128)(2,1)S(1)}, u32[]{:S(2)}, u32[]{:S(2)}) collective-permute-start(bf16[8,9216]{1,0:T(8,128)(2,1)S(1)} %get-tuple-element.16), channel_id=1, source_target_pairs={{0,3},{1,2},{2,1},{3,0},{4,7},{5,6},{6,5},{7,4},{8,11},{9,10},{10,... | collective-permute-start | bytes 442376 | tf_op jit(solution)/shard_map/ppermute | solution.py:207
  24.9 9.3 %collective-permute-start.4 = (bf16[8,9216]{1,0:T(8,128)(2,1)S(1)}, bf16[8,9216]{1,0:T(8,128)(2,1)S(1)}, u32[]{:S(2)}, u32[]{:S(2)}) collective-permute-start(bf16[8,9216]{1,0:T(8,128)(2,1)S(1)} %get-tuple-element.15), channel_id=1, source_target_pairs={{0,2},{1,3},{2,0},{3,1},{4,6},{5,7},{6,4},{7,5},{8,10},{9,11},{10,... | collective-permute-start | bytes 442376 | tf_op jit(solution)/shard_map/ppermute | solution.py:207
  26.5 7.7 %collective-permute-start.3 = (bf16[8,9216]{1,0:T(8,128)(2,1)S(1)}, bf16[8,9216]{1,0:T(8,128)(2,1)S(1)}, u32[]{:S(2)}, u32[]{:S(2)}) collective-permute-start(bf16[8,9216]{1,0:T(8,128)(2,1)S(1)} %get-tuple-element.14), channel_id=1, source_target_pairs={{0,1},{1,0},{2,3},{3,2},{4,5},{5,4},{6,7},{7,6},{8,9},{9,8},{10,11... | collective-permute-start | bytes 442376 | tf_op jit(solution)/shard_map/ppermute | solution.py:207
  31.0 11.1 %collective-permute-start.8 = (bf16[4,32,1024]{2,1,0:T(8,128)(2,1)S(1)}, bf16[4,32,1024]{2,1,0:T(8,128)(2,1)S(1)}, u32[]{:S(2)}, u32[]{:S(2)}) collective-permute-start(bf16[4,32,1024]{2,1,0:T(8,128)(2,1)S(1)} %get-tuple-element.9.rest_0_), channel_id=1, source_target_pairs={{0,12},{4,8},{8,4},{12,0},{1,13},{5,9},{9,5},{13,1},{2,14},{6,10},... | collective-permute-start | bytes 786440 | tf_op jit(solution)/shard_map/ppermute | solution.py:207
  34.2 25.1 %collective-permute-start.9 = (bf16[4,32,1024]{2,1,0:T(8,128)(2,1)S(1)}, bf16[4,32,1024]{2,1,0:T(8,128)(2,1)S(1)}, u32[]{:S(2)}, u32[]{:S(2)}) collective-permute-start(bf16[4,32,1024]{2,1,0:T(8,128)(2,1)S(1)} %get-tuple-element.8.rest_1_), channel_id=1, source_target_pairs={{0,4},{4,0},{8,12},{12,8},{1,5},{5,1},{9,13},{13,9},{2,6},{6,2},{1... | collective-permute-start | bytes 786440 | tf_op jit(solution)/shard_map/ppermute | solution.py:207
  34.2 27.8 %collective-permute-start.10 = (bf16[4,32,1024]{2,1,0:T(8,128)(2,1)S(1)}, bf16[4,32,1024]{2,1,0:T(8,128)(2,1)S(1)}, u32[]{:S(2)}, u32[]{:S(2)}) collective-permute-start(bf16[4,32,1024]{2,1,0:T(8,128)(2,1)S(1)} %get-tuple-element.8.rest_1_), channel_id=1, source_target_pairs={{0,8},{4,12},{8,0},{12,4},{1,9},{5,13},{9,1},{13,5},{2,10},{6,14},... | collective-permute-start | bytes 786440 | tf_op jit(solution)/shard_map/ppermute | solution.py:207
  37.2 4.8 %copy-start.2 = (bf16[4,32,1024]{2,1,0:T(8,128)(2,1)}, bf16[4,32,1024]{2,1,0:T(8,128)(2,1)S(1)}, u32[]{:S(2)}) copy-start(bf16[4,32,1024]{2,1,0:T(8,128)(2,1)S(1)} %collective-permute-done.6.rest_1_) | copy-start | bytes 786436
  37.2 24.7 %collective-permute-start.11 = (bf16[4,32,1024]{2,1,0:T(8,128)(2,1)S(1)}, bf16[4,32,1024]{2,1,0:T(8,128)(2,1)S(1)}, u32[]{:S(2)}, u32[]{:S(2)}) collective-permute-start(bf16[4,32,1024]{2,1,0:T(8,128)(2,1)S(1)} %get-tuple-element.8.rest_1_), channel_id=1, source_target_pairs={{0,12},{4,8},{8,4},{12,0},{1,13},{5,9},{9,5},{13,1},{2,14},{6,10},... | collective-permute-start | bytes 786440 | tf_op jit(solution)/shard_map/ppermute | solution.py:207
  39.5 2.5 %copy-start.3 = (bf16[4,32,1024]{2,1,0:T(8,128)(2,1)}, bf16[4,32,1024]{2,1,0:T(8,128)(2,1)S(1)}, u32[]{:S(2)}) copy-start(bf16[4,32,1024]{2,1,0:T(8,128)(2,1)S(1)} %collective-permute-done.7.rest_2_) | copy-start | bytes 786436
  42.1 0.7 copy-start.6
  59.3 2.7 %copy-start.4 = (bf16[4,32,1024]{2,1,0:T(8,128)(2,1)}, bf16[4,32,1024]{2,1,0:T(8,128)(2,1)S(1)}, u32[]{:S(2)}) copy-start(bf16[4,32,1024]{2,1,0:T(8,128)(2,1)S(1)} %collective-permute-done.9.rest_2_) | copy-start | bytes 786436
  62.0 0.7 copy-start.5
  62.0 0.8 copy-start.7
  79.5 1.4 %collective-permute-start.12 = (f32[4,128]{1,0:T(4,128)}, f32[4,128]{1,0:T(4,128)S(1)}, u32[]{:S(2)}, u32[]{:S(2)}) collective-permute-start(f32[4,128]{1,0:T(4,128)} %shard_map.96), channel_id=1, source_target_pairs={{0,1},{1,0},{2,3},{3,2},{4,5},{5,4},{6,7},{7,6},{8,9},{9,8},{10,11... | collective-permute-start | bytes 6152 | tf_op jit(solution)/shard_map/ppermute | solution.py:292
  81.6 3.6 %collective-permute-start.13 = (f32[4,128]{1,0:T(4,128)S(1)}, f32[4,128]{1,0:T(4,128)S(1)}, u32[]{:S(2)}, u32[]{:S(2)}) collective-permute-start(f32[4,128]{1,0:T(4,128)S(1)} %add.238), channel_id=1, source_target_pairs={{0,2},{1,3},{2,0},{3,1},{4,6},{5,7},{6,4},{7,5},{8,10},{9,11},{10,... | collective-permute-start | bytes 6152 | tf_op jit(solution)/shard_map/ppermute | solution.py:292
  85.2 15.4 %collective-permute-start.14 = (f32[4,128]{1,0:T(4,128)S(1)}, f32[4,128]{1,0:T(4,128)S(1)}, u32[]{:S(2)}, u32[]{:S(2)}) collective-permute-start(f32[4,128]{1,0:T(4,128)S(1)} %add.239), channel_id=1, source_target_pairs={{0,4},{4,0},{8,12},{12,8},{1,5},{5,1},{9,13},{13,9},{2,6},{6,2},{1... | collective-permute-start | bytes 6152 | tf_op jit(solution)/shard_map/ppermute | solution.py:292
  100.6 4.6 %collective-permute-start.15 = (f32[4,128]{1,0:T(4,128)S(1)}, f32[4,128]{1,0:T(4,128)S(1)}, u32[]{:S(2)}, u32[]{:S(2)}) collective-permute-start(f32[4,128]{1,0:T(4,128)S(1)} %add.240), channel_id=1, source_target_pairs={{0,8},{4,12},{8,0},{12,4},{1,9},{5,13},{9,1},{13,5},{2,10},{6,14},... | collective-permute-start | bytes 6152 | tf_op jit(solution)/shard_map/ppermute | solution.py:292
  105.2 0.7 copy-start.9
where the time goes:
time: 107 us; the launch traced here: 106 us
  starting transfers between devices  37.3 us (35%)
  Pallas kernels  33.2 us (31%)
  waiting for transfers between devices  17.6 us (16%)
  other arithmetic  9.12 us (9%)
  local copies, waits for them, and re-layouts  7.65 us (7%)
    pallas_call x2, Pallas kernels, score_part(): pl.pallas_call(kernel, in_specs=[pl.BlockSpec(memory_space=pltpu.SMEM)] *...  33.2 us
    ppermute x12, starting transfers between devices, exchange(): got.append(lax.ppermute(payload, axis, [(s, s ^ k) for s in range(n)]))  19 us
    ppermute x4, starting transfers between devices, scores_of(): scores = scores + lax.ppermute(scores, axis, [(s, s ^ k) for s in range(n)])  18.3 us
    ppermute x12, waiting for transfers between devices, exchange(): got.append(lax.ppermute(payload, axis, [(s, s ^ k) for s in range(n)]))  10.9 us
    ppermute x4, waiting for transfers between devices, scores_of(): scores = scores + lax.ppermute(scores, axis, [(s, s ^ k) for s in range(n)])  6.72 us
  transfers between devices with their start and end apart: 16, of which 9 were waited for; matrix products, arithmetic and copies ran while one was open for 12% of the time, Pallas kernels for 16%

commit v1 on v0

--- a/solution.py
+++ b/solution.py
@@ -12,8 +12,8 @@
 BLOCK = 128
 SEQS = 4
 UNROLL = 16
-CHUNKS = 2
 FLIGHT = 4
+FIRST_SHARE = 9
 SLOT_BITS = 10
 
 damping = 0.1
@@ -130,10 +130,16 @@
         out_ref[q : q + 1, :] = base_ref[q : q + 1, :] + mapped if has_base else mapped
 
 
-def block_lists(mask, unit, piece, chunks):
+def block_lists(mask, unit, piece, blocks):
     queries, row_units, _ = mask.shape
-    mask = mask.reshape(queries, row_units, chunks, -1).transpose(2, 1, 0, 3)
-    col_blocks = mask.shape[3]
+    chunks, col_blocks = len(blocks), max(blocks)
+    begins = [sum(blocks[:c]) for c in range(chunks)]
+    mask = jnp.stack(
+        [
+            jnp.pad(mask[:, :, b : b + n], ((0, 0), (0, 0), (0, col_blocks - n)))
+            for b, n in zip(begins, blocks)
+        ]
+    ).transpose(0, 2, 1, 3)
     half = (col_blocks + 1) // 2
     kept = mask.astype(jnp.int32)
     col = jnp.arange(col_blocks, dtype=jnp.int32)
@@ -146,9 +152,10 @@
     has_a, has_b = count > 2 * pair, count > 2 * pair + 1
     row = jnp.arange(row_units, dtype=jnp.int32)[:, None, None]
     query = jnp.arange(queries, dtype=jnp.int32)[:, None]
-    spare = queries * col_blocks
-    slot_a = query * col_blocks + col_a
-    slot_b = jnp.where(has_b, query * col_blocks + col_b, spare)
+    stride = jnp.array(blocks, jnp.int32)[:, None, None, None]
+    spare = queries * stride
+    slot_a = query * stride + col_a
+    slot_b = jnp.where(has_b, query * stride + col_b, spare)
     code = ((row << SLOT_BITS | slot_a) << SLOT_BITS | slot_b) + 1
     code = jnp.where(has_a, code, 0).reshape(chunks, -1)
     entries = code.shape[1]
@@ -158,6 +165,7 @@
     place = jnp.where(code > 0, place, -1)
     slots = jnp.arange(length, dtype=jnp.int32)
     packed = jnp.sum(jnp.where(place[:, None, :] == slots[:, None], code[:, None, :], 0), axis=2)
+    spare = spare[:, :, 0, 0]
     packed = jnp.where(packed > 0, packed - 1, spare << SLOT_BITS | spare)
     pieces = row_units * unit // piece
     begin = jnp.arange(pieces, dtype=jnp.int32) * (entries // pieces)
@@ -216,8 +224,10 @@
     at_out, at_inp = lax.axis_index("out"), lax.axis_index("inp")
     unit = math.gcd(rows, BLOCK)
     tile = max(t for t in range(unit, 512 + 1, unit) if rows % t == 0 and (t % BLOCK == 0 or t == rows))
-    chunks = CHUNKS if (cols // BLOCK) % CHUNKS == 0 else 1
-    width = cols // chunks
+    first = cols // BLOCK * FIRST_SHARE // 16 * BLOCK
+    widths = (first, cols - first)
+    begins = (0, first)
+    chunks = len(widths)
     row_units = rows // unit
     direct = is_small_power(n_out) and is_small_power(n_inp)
     t = jnp.arange(tokens, dtype=jnp.int32)
@@ -230,7 +240,7 @@
             "out", n_out,
         )
         shards = [
-            exchange(lambda k: query_acts[:, :, c * width : (c + 1) * width], "out", n_out)
+            exchange(lambda k: query_acts[:, :, begins[c] : begins[c] + widths[c]], "out", n_out)
             for c in range(chunks)
         ]
         places = at_out ^ jnp.arange(n_out, dtype=jnp.int32)
@@ -241,9 +251,12 @@
         acts = lax.dynamic_slice_in_dim(whole_acts, at_inp * cols, cols, 1)
         near = jnp.concatenate([grads, acts], axis=1)
         whole = lax.all_gather(query_acts, "out", axis=1, tiled=True)
-        shards = [[whole[:, :, c * width : (c + 1) * width]] for c in range(chunks)]
+        shards = [[whole[:, :, begins[c] : begins[c] + widths[c]]] for c in range(chunks)]
         places = jnp.zeros((1,), jnp.int32)
 
+    if direct:
+        near = jnp.concatenate(near, axis=0)
+        near, block_mask = lax.optimization_barrier((near, block_mask))
     if unit < BLOCK:
         query_grads = query_grads.reshape(queries, -1, row_units, unit).transpose(0, 2, 1, 3)
 
@@ -253,10 +266,9 @@
     else:
         band = jnp.take(block_mask, (row_at + unit * jnp.arange(row_units)) // BLOCK, axis=1)
     band = lax.dynamic_slice_in_dim(band, at_inp * (cols // BLOCK), cols // BLOCK, 2) > 0
-    ends, packed = block_lists(band, unit, tile, chunks)
+    ends, packed = block_lists(band, unit, tile, [w // BLOCK for w in widths])
 
     if direct:
-        near = jnp.concatenate(near, axis=0)
         both = exchange(
             lambda k: jnp.concatenate(
                 [near[:, :rows], lax.dynamic_slice_in_dim(near, rows + (at_inp ^ k) * cols, cols, 1)],
@@ -283,7 +295,7 @@
     for c in range(chunks):
         scores = score_part(
             (ends[c], packed[c]), eigen, query_grads, shards[c], places, near, mapping, scores,
-            unit, tile, c * width, width,
+            unit, tile, begins[c], widths[c],
         )
     if direct:
         for axis, n in (("inp", n_inp), ("out", n_out)):

time: 107 us -> 111 us (1.037)
  waiting for transfers between devices: 17.6 us -> 20.4 us
  starting transfers between devices: 37.3 us -> 38.7 us
  local copies, waits for them, and re-layouts: 7.65 us -> 8.79 us
    ppermute x12, waiting for transfers between devices: 10.9 us -> 13.7 us  [exchange(): got.append(lax.ppermute(payload, axis, [(s, s ^ k) for s in range(n)]))]
    ppermute x4, starting transfers between devices: 18.3 us -> 19.7 us  [scores_of(): scores = scores + lax.ppermute(scores, axis, [(s, s ^ k) for s in range(n)])]
  transfers between devices with their start and end apart: 16 -> 16, of which waited for: 9 -> 10; matrix products, arithmetic and copies ran while one was open for 12% -> 12% of each run, Pallas kernels for 16% -> 16%
where the time goes in v1:
time: 111 us; the launch traced here: 110 us
  starting transfers between devices  38.7 us (35%)
  Pallas kernels  32.3 us (29%)
  waiting for transfers between devices  20.4 us (18%)
  other arithmetic  8.86 us (8%)
  local copies, waits for them, and re-layouts  8.79 us (8%)
    pallas_call x2, Pallas kernels, score_part(): pl.pallas_call(kernel, in_specs=[pl.BlockSpec(memory_space=pltpu.SMEM)] *...  32.3 us
    ppermute x4, starting transfers between devices, scores_of(): scores = scores + lax.ppermute(scores, axis, [(s, s ^ k) for s in range(n)])  19.7 us
    ppermute x12, starting transfers between devices, exchange(): got.append(lax.ppermute(payload, axis, [(s, s ^ k) for s in range(n)]))  19 us
    ppermute x12, waiting for transfers between devices, exchange(): got.append(lax.ppermute(payload, axis, [(s, s ^ k) for s in range(n)]))  13.7 us
    ppermute x4, waiting for transfers between devices, scores_of(): scores = scores + lax.ppermute(scores, axis, [(s, s ^ k) for s in range(n)])  6.71 us
  transfers between devices with their start and end apart: 16, of which 10 were waited for; matrix products, arithmetic and copies ran while one was open for 12% of the time, Pallas kernels for 16%

profile of v1, /device:TPU:0, one launch (start us, length us, event | category | flops | bytes accessed | tf_op | source)
XLA Modules:
  0.0 110.2 jit_solution(8607416900123692491)
XLA Ops:
  0.7 1.0 slice.49.rest_0_
  1.7 3.1 %collective-permute-start.6 = (bf16[4,32,1152]{2,1,0:T(8,128)(2,1)S(1)}, bf16[4,32,1152]{2,1,0:T(8,128)(2,1)S(1)}, u32[]{:S(2)}, u32[]{:S(2)}) collective-permute-start(bf16[4,32,1152]{2,1,0:T(8,128)(2,1)S(1)} %slice.49.rest_0_), channel_id=1, source_target_pairs={{0,4},{4,0},{8,12},{12,8},{1,5},{5,1},{9,13},{13,9},{2,6},{6,2},{1... | collective-permute-start | bytes 884744 | tf_op jit(solution)/shard_map/ppermute | solution.py:215
  4.8 2.6 %collective-permute-start.7 = (bf16[4,32,1152]{2,1,0:T(8,128)(2,1)S(1)}, bf16[4,32,1152]{2,1,0:T(8,128)(2,1)S(1)}, u32[]{:S(2)}, u32[]{:S(2)}) collective-permute-start(bf16[4,32,1152]{2,1,0:T(8,128)(2,1)S(1)} %slice.49.rest_0_), channel_id=1, source_target_pairs={{0,8},{4,12},{8,0},{12,4},{1,9},{5,13},{9,1},{13,5},{2,10},{6,14},... | collective-permute-start | bytes 884744 | tf_op jit(solution)/shard_map/ppermute | solution.py:215
  7.4 0.9 constant_dynamic-slice_fusion.7
  8.3 0.9 pad_maximum_fusion.5
  9.3 1.9 %collective-permute-start.1 = (bf16[2,15360]{1,0:T(2,128)(2,1)S(1)}, bf16[2,15360]{1,0:T(2,128)(2,1)S(1)}, u32[]{:S(2)}, u32[]{:S(2)}) collective-permute-start(bf16[2,15360]{1,0:T(2,128)(2,1)S(1)} %get-tuple-element.26), channel_id=1, source_target_pairs={{0,8},{4,12},{8,0},{12,4},{1,9},{5,13},{9,1},{13,5},{2,10},{6,14},... | collective-permute-start | bytes 184328 | tf_op jit(solution)/shard_map/ppermute | solution.py:215
  11.2 2.5 %collective-permute-start = (bf16[2,15360]{1,0:T(2,128)(2,1)S(1)}, bf16[2,15360]{1,0:T(2,128)(2,1)S(1)}, u32[]{:S(2)}, u32[]{:S(2)}) collective-permute-start(bf16[2,15360]{1,0:T(2,128)(2,1)S(1)} %get-tuple-element.25), channel_id=1, source_target_pairs={{0,4},{4,0},{8,12},{12,8},{1,5},{5,1},{9,13},{13,9},{2,6},{6,2},{1... | collective-permute-start | bytes 184328 | tf_op jit(solution)/shard_map/ppermute | solution.py:215
  13.7 0.5 iota_xor_fusion.place_ref
  14.2 0.4 iota_compare_fusion.1
  14.6 1.0 slice.50.rest_1_
  16.0 0.2 or.49
  16.3 0.2 gt.85
  17.0 0.7 fusion.2.map_ref
  17.7 5.2 %collective-permute-done.2 = bf16[2,15360]{1,0:T(2,128)(2,1)S(1)} collective-permute-done((bf16[2,15360]{1,0:T(2,128)(2,1)S(1)}, bf16[2,15360]{1,0:T(2,128)(2,1)S(1)}, u32[]{:S(2)}, u32[]{:S(2)}) %collective-permute-start.2) | collective-permute-done | bytes 61472 | tf_op jit(solution)/shard_map/ppermute | solution.py:215
  22.9 3.0 %collective-permute-done.1 = bf16[2,15360]{1,0:T(2,128)(2,1)S(1)} collective-permute-done((bf16[2,15360]{1,0:T(2,128)(2,1)S(1)}, bf16[2,15360]{1,0:T(2,128)(2,1)S(1)}, u32[]{:S(2)}, u32[]{:S(2)}) %collective-permute-start.1) | collective-permute-done | bytes 61472 | tf_op jit(solution)/shard_map/ppermute | solution.py:215
  25.9 0.3 pad_maximum_fusion.1
  27.2 0.3 add.217
  27.7 0.2 gt.83
  28.1 0.2 add.214
  28.5 0.3 fusion
  28.8 1.2 %convert_reduce_fusion = s32[2,1120]{1,0:T(2,128)S(1)} fusion(pred[2,1120]{1,0:T(4,128)(4,1)S(1)} %get-tuple-element.12, pred[1120,1120]{1,0:T(8,128)(4,1)S(1)} %iota_compare_fusion.1), kind=kLoop, calls=%fused_computation.2 | loop fusion | flops 7524160 | bytes 1265600 | tf_op jit(solution)/shard_map/reduce_sum | solution.py:164
  30.2 1.6 %collective-permute-start.4 = (bf16[8,9216]{1,0:T(8,128)(2,1)S(1)}, bf16[8,9216]{1,0:T(8,128)(2,1)S(1)}, u32[]{:S(2)}, u32[]{:S(2)}) collective-permute-start(bf16[8,9216]{1,0:T(8,128)(2,1)S(1)} %get-tuple-element.19), channel_id=1, source_target_pairs={{0,2},{1,3},{2,0},{3,1},{4,6},{5,7},{6,4},{7,5},{8,10},{9,11},{10,... | collective-permute-start | bytes 442376 | tf_op jit(solution)/shard_map/ppermute | solution.py:215
  31.8 0.3 collective-permute-start.3
  32.1 1.6 %select_reduce_fusion = s32[2,1136]{1,0:T(2,128)S(1)} fusion(s32[2,1120]{1,0:T(2,128)S(1)} %get-tuple-element.13, s32[2,1120]{1,0:T(2,128)S(1)} %broadcast_select_fusion.1), kind=kLoop, calls=%fused_computation | loop fusion | flops 7631648 | bytes 27008 | tf_op jit(solution)/shard_map/reduce_sum | solution.py:167
  33.9 0.8 slice_reduce_fusion
  34.6 0.6 slice_reduce_fusion.2
  35.2 1.1 %collective-permute-done.5 = bf16[8,9216]{1,0:T(8,128)(2,1)S(1)} collective-permute-done((bf16[8,9216]{1,0:T(8,128)(2,1)S(1)}, bf16[8,9216]{1,0:T(8,128)(2,1)S(1)}, u32[]{:S(2)}, u32[]{:S(2)}) %collective-permute-start.5) | collective-permute-done | bytes 147488 | tf_op jit(solution)/shard_map/ppermute | solution.py:215
  36.3 2.5 %collective-permute-start.8 = (bf16[4,32,1152]{2,1,0:T(8,128)(2,1)S(1)}, bf16[4,32,1152]{2,1,0:T(8,128)(2,1)S(1)}, u32[]{:S(2)}, u32[]{:S(2)}) collective-permute-start(bf16[4,32,1152]{2,1,0:T(8,128)(2,1)S(1)} %slice.49.rest_0_), channel_id=1, source_target_pairs={{0,12},{4,8},{8,4},{12,0},{1,13},{5,9},{9,5},{13,1},{2,14},{6,10},... | collective-permute-start | bytes 884744 | tf_op jit(solution)/shard_map/ppermute | solution.py:215
  38.8 0.7 collective-permute-done.4
  39.6 3.0 %collective-permute-start.10 = (bf16[4,32,896]{2,1,0:T(8,128)(2,1)S(1)}, bf16[4,32,896]{2,1,0:T(8,128)(2,1)S(1)}, u32[]{:S(2)}, u32[]{:S(2)}) collective-permute-start(bf16[4,32,896]{2,1,0:T(8,128)(2,1)S(1)} %slice.50.rest_1_), channel_id=1, source_target_pairs={{0,8},{4,12},{8,0},{12,4},{1,9},{5,13},{9,1},{13,5},{2,10},{6,14},... | collective-permute-start | bytes 688136 | tf_op jit(solution)/shard_map/ppermute | solution.py:215
  42.6 1.4 %collective-permute-start.11 = (bf16[4,32,896]{2,1,0:T(8,128)(2,1)S(1)}, bf16[4,32,896]{2,1,0:T(8,128)(2,1)S(1)}, u32[]{:S(2)}, u32[]{:S(2)}) collective-permute-start(bf16[4,32,896]{2,1,0:T(8,128)(2,1)S(1)} %slice.50.rest_1_), channel_id=1, source_target_pairs={{0,12},{4,8},{8,4},{12,0},{1,13},{5,9},{9,5},{13,1},{2,14},{6,10},... | collective-permute-start | bytes 688136 | tf_op jit(solution)/shard_map/ppermute | solution.py:215
  44.0 0.9 pad_maximum_fusion.near_ref
  44.9 3.2 %collective-permute-done.8.rest_3_ = bf16[4,32,1152]{2,1,0:T(8,128)(2,1)S(1)} collective-permute-done((bf16[4,32,1152]{2,1,0:T(8,128)(2,1)S(1)}, bf16[4,32,1152]{2,1,0:T(8,128)(2,1)S(1)}, u32[]{:S(2)}, u32[]{:S(2)}) %collective-permute-start.8) | collective-permute-done | bytes 294944 | tf_op jit(solution)/shard_map/ppermute | solution.py:215
  48.1 0.7 copy-done.4
  48.8 17.3 %shard_map.104.rest_0_ = f32[4,128]{1,0:T(4,128)} custom-call(s32[4]{0:T(128)} %iota_xor_fusion.place_ref, s32[14]{0:T(128)} %get-tuple-element.10.end_ref, s32[1136]{0:T(1024)} %get-tuple-element.8.packed_ref, bf16[7168,2048]{1,0:T(8,128)(2,1)} %eigen_hbm.3, bf16[4,128,7168]{2,1,0:T(8,128)(2,1)} %queries_hbm.3, bf16[32,9216]{1,0:T(8,128)(2,1)} %pad_maximum_fusion.near_ref, ...), custom_call_target="tpu_custom_call" | custom-call | tf_op jit(solution)/shard_map/pallas_call | solution.py:189
  66.2 0.5 collective-permute-done.10.rest_3_
  66.6 0.2 copy-done.6
  66.8 0.5 copy-done.7
  67.4 15.0 %shard_map.105 = f32[4,128]{1,0:T(4,128)} custom-call(s32[4]{0:T(128)} %iota_xor_fusion.place_ref, s32[14]{0:T(128)} %get-tuple-element.11.end_ref, s32[1136]{0:T(1024)} %get-tuple-element.9.packed_ref, bf16[7168,2048]{1,0:T(8,128)(2,1)} %eigen_hbm.3, bf16[4,128,7168]{2,1,0:T(8,128)(2,1)} %queries_hbm.3, bf16[32,9216]{1,0:T(8,128)(2,1)} %pad_maximum_fusion.near_ref, ...), custom_call_target="tpu_custom_call" | custom-call | tf_op jit(solution)/shard_map/pallas_call | solution.py:189
  82.5 1.4 %collective-permute-done.12 = f32[4,128]{1,0:T(4,128)S(1)} collective-permute-done((f32[4,128]{1,0:T(4,128)}, f32[4,128]{1,0:T(4,128)S(1)}, u32[]{:S(2)}, u32[]{:S(2)}) %collective-permute-start.12) | collective-permute-done | bytes 2080 | tf_op jit(solution)/shard_map/ppermute | solution.py:304
  83.9 0.7 add.234
  84.5 1.4 %collective-permute-start.13 = (f32[4,128]{1,0:T(4,128)S(1)}, f32[4,128]{1,0:T(4,128)S(1)}, u32[]{:S(2)}, u32[]{:S(2)}) collective-permute-start(f32[4,128]{1,0:T(4,128)S(1)} %add.234), channel_id=1, source_target_pairs={{0,2},{1,3},{2,0},{3,1},{4,6},{5,7},{6,4},{7,5},{8,10},{9,11},{10,... | collective-permute-start | bytes 6152 | tf_op jit(solution)/shard_map/ppermute | solution.py:304
  85.9 2.2 %collective-permute-done.13 = f32[4,128]{1,0:T(4,128)S(1)} collective-permute-done((f32[4,128]{1,0:T(4,128)S(1)}, f32[4,128]{1,0:T(4,128)S(1)}, u32[]{:S(2)}, u32[]{:S(2)}) %collective-permute-start.13) | collective-permute-done | bytes 2080 | tf_op jit(solution)/shard_map/ppermute | solution.py:304
  88.1 15.2 %collective-permute-start.14 = (f32[4,128]{1,0:T(4,128)S(1)}, f32[4,128]{1,0:T(4,128)S(1)}, u32[]{:S(2)}, u32[]{:S(2)}) collective-permute-start(f32[4,128]{1,0:T(4,128)S(1)} %add.235), channel_id=1, source_target_pairs={{0,4},{4,0},{8,12},{12,8},{1,5},{5,1},{9,13},{13,9},{2,6},{6,2},{1... | collective-permute-start | bytes 6152 | tf_op jit(solution)/shard_map/ppermute | solution.py:304
  103.4 1.6 %collective-permute-done.14 = f32[4,128]{1,0:T(4,128)S(1)} collective-permute-done((f32[4,128]{1,0:T(4,128)S(1)}, f32[4,128]{1,0:T(4,128)S(1)}, u32[]{:S(2)}, u32[]{:S(2)}) %collective-permute-start.14) | collective-permute-done | bytes 2080 | tf_op jit(solution)/shard_map/ppermute | solution.py:304
  104.9 3.0 %collective-permute-start.15 = (f32[4,128]{1,0:T(4,128)S(1)}, f32[4,128]{1,0:T(4,128)S(1)}, u32[]{:S(2)}, u32[]{:S(2)}) collective-permute-start(f32[4,128]{1,0:T(4,128)S(1)} %add.236), channel_id=1, source_target_pairs={{0,8},{4,12},{8,0},{12,4},{1,9},{5,13},{9,1},{13,5},{2,10},{6,14},... | collective-permute-start | bytes 6152 | tf_op jit(solution)/shard_map/ppermute | solution.py:304
  108.0 1.6 %collective-permute-done.15 = f32[4,128]{1,0:T(4,128)S(1)} collective-permute-done((f32[4,128]{1,0:T(4,128)S(1)}, f32[4,128]{1,0:T(4,128)S(1)}, u32[]{:S(2)}, u32[]{:S(2)}) %collective-permute-start.15) | collective-permute-done | bytes 2080 | tf_op jit(solution)/shard_map/ppermute | solution.py:304
  109.5 0.6 slice.52
  (77 shorter events, 3.0 us)
Async XLA Ops:
  0.6 15.0 %copy-start.15 = (s32[2]{0:T(128)S(1)}, s32[2]{0:T(128)}, u32[]{:S(2)}) copy-start(s32[2]{0:T(128)} %constant.157.clone) | copy-start | bytes 28
  0.6 25.2 %copy-start.9 = (bf16[2,8192]{1,0:T(2,128)(2,1)S(1)}, bf16[2,8192]{1,0:T(2,128)(2,1)}, u32[]{:S(2)}) copy-start(bf16[2,8192]{1,0:T(2,128)(2,1)} %param.9) | copy-start | bytes 98308
  0.7 15.9 %copy-start.13 = (s32[32]{0:T(128)S(1)}, s32[32]{0:T(128)}, u32[]{:S(2)}) copy-start(s32[32]{0:T(128)} %param.15) | copy-start | bytes 388
  0.7 16.1 %copy-start.14 = (s32[32]{0:T(128)S(1)}, s32[32]{0:T(128)}, u32[]{:S(2)}) copy-start(s32[32]{0:T(128)} %param.16) | copy-start | bytes 388
  0.7 25.5 %copy-start.5 = (s32[4,224,64]{1,2,0:T(8,128)S(1)}, s32[4,224,64]{1,2,0:T(8,128)}, u32[]{:S(2)}) copy-start(s32[4,224,64]{1,2,0:T(8,128)} %param.14) | copy-start | bytes 688132
  1.7 34.6 %copy-start = (bf16[4,32,1152]{2,1,0:T(8,128)(2,1)}, bf16[4,32,1152]{2,1,0:T(8,128)(2,1)S(1)}, u32[]{:S(2)}) copy-start(bf16[4,32,1152]{2,1,0:T(8,128)(2,1)S(1)} %slice.49.rest_0_) | copy-start | bytes 884740
  1.7 40.9 %collective-permute-start.6 = (bf16[4,32,1152]{2,1,0:T(8,128)(2,1)S(1)}, bf16[4,32,1152]{2,1,0:T(8,128)(2,1)S(1)}, u32[]{:S(2)}, u32[]{:S(2)}) collective-permute-start(bf16[4,32,1152]{2,1,0:T(8,128)(2,1)S(1)} %slice.49.rest_0_), channel_id=1, source_target_pairs={{0,4},{4,0},{8,12},{12,8},{1,5},{5,1},{9,13},{13,9},{2,6},{6,2},{1... | collective-permute-start | bytes 884744 | tf_op jit(solution)/shard_map/ppermute | solution.py:215
  4.8 40.0 %collective-permute-start.7 = (bf16[4,32,1152]{2,1,0:T(8,128)(2,1)S(1)}, bf16[4,32,1152]{2,1,0:T(8,128)(2,1)S(1)}, u32[]{:S(2)}, u32[]{:S(2)}) collective-permute-start(bf16[4,32,1152]{2,1,0:T(8,128)(2,1)S(1)} %slice.49.rest_0_), channel_id=1, source_target_pairs={{0,8},{4,12},{8,0},{12,4},{1,9},{5,13},{9,1},{13,5},{2,10},{6,14},... | collective-permute-start | bytes 884744 | tf_op jit(solution)/shard_map/ppermute | solution.py:215
  9.2 13.6 %collective-permute-start.2 = (bf16[2,15360]{1,0:T(2,128)(2,1)S(1)}, bf16[2,15360]{1,0:T(2,128)(2,1)S(1)}, u32[]{:S(2)}, u32[]{:S(2)}) collective-permute-start(bf16[2,15360]{1,0:T(2,128)(2,1)S(1)} %get-tuple-element.27), channel_id=1, source_target_pairs={{0,12},{4,8},{8,4},{12,0},{1,13},{5,9},{9,5},{13,1},{2,14},{6,10},... | collective-permute-start | bytes 184328 | tf_op jit(solution)/shard_map/ppermute | solution.py:215
  9.3 16.6 %collective-permute-start.1 = (bf16[2,15360]{1,0:T(2,128)(2,1)S(1)}, bf16[2,15360]{1,0:T(2,128)(2,1)S(1)}, u32[]{:S(2)}, u32[]{:S(2)}) collective-permute-start(bf16[2,15360]{1,0:T(2,128)(2,1)S(1)} %get-tuple-element.26), channel_id=1, source_target_pairs={{0,8},{4,12},{8,0},{12,4},{1,9},{5,13},{9,1},{13,5},{2,10},{6,14},... | collective-permute-start | bytes 184328 | tf_op jit(solution)/shard_map/ppermute | solution.py:215
  11.2 14.7 %collective-permute-start = (bf16[2,15360]{1,0:T(2,128)(2,1)S(1)}, bf16[2,15360]{1,0:T(2,128)(2,1)S(1)}, u32[]{:S(2)}, u32[]{:S(2)}) collective-permute-start(bf16[2,15360]{1,0:T(2,128)(2,1)S(1)} %get-tuple-element.25), channel_id=1, source_target_pairs={{0,4},{4,0},{8,12},{12,8},{1,5},{5,1},{9,13},{13,9},{2,6},{6,2},{1... | collective-permute-start | bytes 184328 | tf_op jit(solution)/shard_map/ppermute | solution.py:215
  14.2 14.2 %copy-start.11 = (s32[2]{0:T(128)S(1)}, s32[2]{0:T(128)}, u32[]{:S(2)}) copy-start(s32[2]{0:T(128)} %constant.162) | copy-start | bytes 28
  15.6 27.0 %copy-start.1 = (bf16[4,32,896]{2,1,0:T(8,128)(2,1)}, bf16[4,32,896]{2,1,0:T(8,128)(2,1)S(1)}, u32[]{:S(2)}) copy-start(bf16[4,32,896]{2,1,0:T(8,128)(2,1)S(1)} %slice.50.rest_1_) | copy-start | bytes 688132
  26.2 7.5 %copy-start.12 = (s32[2]{0:T(128)S(1)}, s32[2]{0:T(128)}, u32[]{:S(2)}) copy-start(s32[2]{0:T(128)} %constant.164) | copy-start | bytes 28
  30.2 6.2 %collective-permute-start.5 = (bf16[8,9216]{1,0:T(8,128)(2,1)S(1)}, bf16[8,9216]{1,0:T(8,128)(2,1)S(1)}, u32[]{:S(2)}, u32[]{:S(2)}) collective-permute-start(bf16[8,9216]{1,0:T(8,128)(2,1)S(1)} %get-tuple-element.20), channel_id=1, source_target_pairs={{0,3},{1,2},{2,1},{3,0},{4,7},{5,6},{6,5},{7,4},{8,11},{9,10},{10,... | collective-permute-start | bytes 442376 | tf_op jit(solution)/shard_map/ppermute | solution.py:215
  30.2 9.3 %collective-permute-start.4 = (bf16[8,9216]{1,0:T(8,128)(2,1)S(1)}, bf16[8,9216]{1,0:T(8,128)(2,1)S(1)}, u32[]{:S(2)}, u32[]{:S(2)}) collective-permute-start(bf16[8,9216]{1,0:T(8,128)(2,1)S(1)} %get-tuple-element.19), channel_id=1, source_target_pairs={{0,2},{1,3},{2,0},{3,1},{4,6},{5,7},{6,4},{7,5},{8,10},{9,11},{10,... | collective-permute-start | bytes 442376 | tf_op jit(solution)/shard_map/ppermute | solution.py:215
  31.8 7.7 %collective-permute-start.3 = (bf16[8,9216]{1,0:T(8,128)(2,1)S(1)}, bf16[8,9216]{1,0:T(8,128)(2,1)S(1)}, u32[]{:S(2)}, u32[]{:S(2)}) collective-permute-start(bf16[8,9216]{1,0:T(8,128)(2,1)S(1)} %get-tuple-element.18), channel_id=1, source_target_pairs={{0,1},{1,0},{2,3},{3,2},{4,5},{5,4},{6,7},{7,6},{8,9},{9,8},{10,11... | collective-permute-start | bytes 442376 | tf_op jit(solution)/shard_map/ppermute | solution.py:215
  36.3 11.8 %collective-permute-start.8 = (bf16[4,32,1152]{2,1,0:T(8,128)(2,1)S(1)}, bf16[4,32,1152]{2,1,0:T(8,128)(2,1)S(1)}, u32[]{:S(2)}, u32[]{:S(2)}) collective-permute-start(bf16[4,32,1152]{2,1,0:T(8,128)(2,1)S(1)} %slice.49.rest_0_), channel_id=1, source_target_pairs={{0,12},{4,8},{8,4},{12,0},{1,13},{5,9},{9,5},{13,1},{2,14},{6,10},... | collective-permute-start | bytes 884744 | tf_op jit(solution)/shard_map/ppermute | solution.py:215
  39.5 26.6 %collective-permute-start.9 = (bf16[4,32,896]{2,1,0:T(8,128)(2,1)S(1)}, bf16[4,32,896]{2,1,0:T(8,128)(2,1)S(1)}, u32[]{:S(2)}, u32[]{:S(2)}) collective-permute-start(bf16[4,32,896]{2,1,0:T(8,128)(2,1)S(1)} %slice.50.rest_1_), channel_id=1, source_target_pairs={{0,4},{4,0},{8,12},{12,8},{1,5},{5,1},{9,13},{13,9},{2,6},{6,2},{1... | collective-permute-start | bytes 688136 | tf_op jit(solution)/shard_map/ppermute | solution.py:215
  39.6 27.1 %collective-permute-start.10 = (bf16[4,32,896]{2,1,0:T(8,128)(2,1)S(1)}, bf16[4,32,896]{2,1,0:T(8,128)(2,1)S(1)}, u32[]{:S(2)}, u32[]{:S(2)}) collective-permute-start(bf16[4,32,896]{2,1,0:T(8,128)(2,1)S(1)} %slice.50.rest_1_), channel_id=1, source_target_pairs={{0,8},{4,12},{8,0},{12,4},{1,9},{5,13},{9,1},{13,5},{2,10},{6,14},... | collective-permute-start | bytes 688136 | tf_op jit(solution)/shard_map/ppermute | solution.py:215
  42.6 5.5 %copy-start.2 = (bf16[4,32,1152]{2,1,0:T(8,128)(2,1)}, bf16[4,32,1152]{2,1,0:T(8,128)(2,1)S(1)}, u32[]{:S(2)}) copy-start(bf16[4,32,1152]{2,1,0:T(8,128)(2,1)S(1)} %collective-permute-done.6.rest_1_) | copy-start | bytes 884740
  42.6 24.0 %collective-permute-start.11 = (bf16[4,32,896]{2,1,0:T(8,128)(2,1)S(1)}, bf16[4,32,896]{2,1,0:T(8,128)(2,1)S(1)}, u32[]{:S(2)}, u32[]{:S(2)}) collective-permute-start(bf16[4,32,896]{2,1,0:T(8,128)(2,1)S(1)} %slice.50.rest_1_), channel_id=1, source_target_pairs={{0,12},{4,8},{8,4},{12,0},{1,13},{5,9},{9,5},{13,1},{2,14},{6,10},... | collective-permute-start | bytes 688136 | tf_op jit(solution)/shard_map/ppermute | solution.py:215
  44.9 3.2 %copy-start.3 = (bf16[4,32,1152]{2,1,0:T(8,128)(2,1)}, bf16[4,32,1152]{2,1,0:T(8,128)(2,1)S(1)}, u32[]{:S(2)}) copy-start(bf16[4,32,1152]{2,1,0:T(8,128)(2,1)S(1)} %collective-permute-done.7.rest_2_) | copy-start | bytes 884740
  48.1 0.7 copy-start.4
  66.2 0.7 copy-start.6
  66.6 0.7 copy-start.7
  66.6 0.8 copy-start.8
  82.4 1.4 %collective-permute-start.12 = (f32[4,128]{1,0:T(4,128)}, f32[4,128]{1,0:T(4,128)S(1)}, u32[]{:S(2)}, u32[]{:S(2)}) collective-permute-start(f32[4,128]{1,0:T(4,128)} %shard_map.105), channel_id=1, source_target_pairs={{0,1},{1,0},{2,3},{3,2},{4,5},{5,4},{6,7},{7,6},{8,9},{9,8},{10,11... | collective-permute-start | bytes 6152 | tf_op jit(solution)/shard_map/ppermute | solution.py:304
  84.5 3.6 %collective-permute-start.13 = (f32[4,128]{1,0:T(4,128)S(1)}, f32[4,128]{1,0:T(4,128)S(1)}, u32[]{:S(2)}, u32[]{:S(2)}) collective-permute-start(f32[4,128]{1,0:T(4,128)S(1)} %add.234), channel_id=1, source_target_pairs={{0,2},{1,3},{2,0},{3,1},{4,6},{5,7},{6,4},{7,5},{8,10},{9,11},{10,... | collective-permute-start | bytes 6152 | tf_op jit(solution)/shard_map/ppermute | solution.py:304
  88.1 16.8 %collective-permute-start.14 = (f32[4,128]{1,0:T(4,128)S(1)}, f32[4,128]{1,0:T(4,128)S(1)}, u32[]{:S(2)}, u32[]{:S(2)}) collective-permute-start(f32[4,128]{1,0:T(4,128)S(1)} %add.235), channel_id=1, source_target_pairs={{0,4},{4,0},{8,12},{12,8},{1,5},{5,1},{9,13},{13,9},{2,6},{6,2},{1... | collective-permute-start | bytes 6152 | tf_op jit(solution)/shard_map/ppermute | solution.py:304
  104.9 4.6 %collective-permute-start.15 = (f32[4,128]{1,0:T(4,128)S(1)}, f32[4,128]{1,0:T(4,128)S(1)}, u32[]{:S(2)}, u32[]{:S(2)}) collective-permute-start(f32[4,128]{1,0:T(4,128)S(1)} %add.236), channel_id=1, source_target_pairs={{0,8},{4,12},{8,0},{12,4},{1,9},{5,13},{9,1},{13,5},{2,10},{6,14},... | collective-permute-start | bytes 6152 | tf_op jit(solution)/shard_map/ppermute | solution.py:304
  109.5 0.7 copy-start.10

commit v2 on v1

--- a/solution.py
+++ b/solution.py
@@ -11,9 +11,9 @@
 
 BLOCK = 128
 SEQS = 4
-UNROLL = 16
+UNROLL = 24
 FLIGHT = 4
-FIRST_SHARE = 9
+FIRST_SHARE = 8
 SLOT_BITS = 10
 
 damping = 0.1
@@ -76,21 +76,23 @@
         row, slot_a, slot_b = entry(at)
         query = jnp.minimum(lax.div(slot_a, col_blocks), queries - 1)
         rows_at = pl.ds(pl.multiple_of(row * unit, unit), unit)
-        right = jnp.concatenate([weights_ref[slot_a], weights_ref[slot_b]], axis=1)
         left = queries_ref[query, :, rows_at] if unit == BLOCK else queries_ref[query, row]
+        right = jnp.concatenate(
+            [weights_ref[slot, : left.shape[0], :] for slot in (slot_a, slot_b)], axis=1
+        )
         outer = lax.dot_general(
             left, right, (((0,), (0,)), ((), ())), preferred_element_type=jnp.float32
         )
         for h, slot in enumerate((slot_a, slot_b)):
             cols = pl.ds(pl.multiple_of(lax.rem(slot, col_blocks) * BLOCK, BLOCK), BLOCK)
             scale = 1.0 / (eigen_ref[rows_at, cols].astype(jnp.float32) + damping)
-            hold[:, h * BLOCK : (h + 1) * BLOCK] = (
+            hold[h] = (
                 outer[:, h * BLOCK : (h + 1) * BLOCK] * scale
             ).astype(jnp.bfloat16)
 
     def add_part(at, hold):
         row, slot_a, slot_b = entry(at)
-        part = jnp.dot(grads_scr[row], hold[...], preferred_element_type=jnp.float32)
+        part = jnp.dot(grads_scr[row], jnp.concatenate([hold[0], hold[1]], axis=1), preferred_element_type=jnp.float32)
         sums_ref[slot_a] += part[:, :BLOCK]
         sums_ref[slot_b] += part[:, BLOCK:]
 
@@ -180,7 +182,7 @@
 def score_part(lists, eigen, query_grads, shards, places, near, mapping, base, unit, piece, first_col, width):
     queries = query_grads.shape[0]
     rows = eigen.shape[0]
-    query_tokens = shards[0].shape[1] * len(shards)
+    token_space = shards[0].shape[1] * len(shards)
     tokens = near.shape[0]
     col_blocks = width // BLOCK
     kernel = functools.partial(score_kernel, unit, piece, first_col, len(shards), base is not None)
@@ -193,11 +195,11 @@
         scratch_shapes=[
             pltpu.VMEM((rows, width), jnp.bfloat16),
             pltpu.VMEM(query_grads.shape, jnp.bfloat16),
-            pltpu.VMEM((queries * col_blocks + 1, query_tokens, BLOCK), jnp.bfloat16),
+            pltpu.VMEM((queries * col_blocks + 1, token_space, BLOCK), jnp.bfloat16),
             pltpu.VMEM((rows // unit, tokens, unit), jnp.bfloat16),
             pltpu.VMEM((queries * col_blocks + 1, tokens, BLOCK), jnp.float32),
             pltpu.SemaphoreType.DMA((2, rows // piece)),
-            *[pltpu.VMEM((unit, 2 * BLOCK), jnp.bfloat16)] * UNROLL,
+            *[pltpu.VMEM((2, unit, BLOCK), jnp.bfloat16)] * UNROLL,
         ],
         out_shape=jax.ShapeDtypeStruct((queries, mapping.shape[1]), jnp.float32),
         compiler_params=pltpu.CompilerParams(vmem_limit_bytes=56 << 20),
@@ -214,6 +216,14 @@
         payload = make(k)
         got.append(lax.ppermute(payload, axis, [(s, s ^ k) for s in range(n)]))
     return got
+
+
+def relay_exchange(mine, axis):
+    far = lax.ppermute(mine, axis, [(0, 2), (2, 0), (1, 3), (3, 1)])
+    near = lax.ppermute(mine, axis, [(0, 1), (1, 0), (2, 3), (3, 2)])
+    middle = lax.ppermute(mine, axis, [(1, 2), (2, 1)])
+    ends = lax.ppermute(far, axis, [(2, 3), (1, 0)])
+    return [mine, near, far, middle, ends]
 
 
 def scores_of(n_out, n_inp, acts_rot, grads_rot, query_grads, query_acts, eigen, block_mask, order, segment_ids):
@@ -239,11 +249,18 @@
             ),
             "out", n_out,
         )
-        shards = [
-            exchange(lambda k: query_acts[:, :, begins[c] : begins[c] + widths[c]], "out", n_out)
-            for c in range(chunks)
-        ]
-        places = at_out ^ jnp.arange(n_out, dtype=jnp.int32)
+        sent = [query_acts[:, :, b : b + w] for b, w in zip(begins, widths)]
+        places = [at_out ^ jnp.arange(n_out, dtype=jnp.int32)] * chunks
+        if n_out == 4:
+            shards = [relay_exchange(sent[0], "out")]
+            other = at_out ^ 3
+            inner = (at_out == 1) | (at_out == 2)
+            places[0] = jnp.stack(
+                [at_out, at_out ^ 1, at_out ^ 2, jnp.where(inner, other, 4), jnp.where(inner, 4, other)]
+            ).astype(jnp.int32)
+        else:
+            shards = [exchange(lambda k: sent[0], "out", n_out)]
+        shards.append(exchange(lambda k: sent[1], "out", n_out))
     else:
         spread = lax.all_to_all(grads_rot[None], "out", split_axis=2, concat_axis=0, tiled=True)
         grads = lax.all_gather(spread, "inp", axis=1, tiled=True).reshape(-1, rows)
@@ -252,7 +269,7 @@
         near = jnp.concatenate([grads, acts], axis=1)
         whole = lax.all_gather(query_acts, "out", axis=1, tiled=True)
         shards = [[whole[:, :, begins[c] : begins[c] + widths[c]]] for c in range(chunks)]
-        places = jnp.zeros((1,), jnp.int32)
+        places = [jnp.zeros((1,), jnp.int32)] * chunks
 
     if direct:
         near = jnp.concatenate(near, axis=0)
@@ -294,7 +311,7 @@
     scores = None
     for c in range(chunks):
         scores = score_part(
-            (ends[c], packed[c]), eigen, query_grads, shards[c], places, near, mapping, scores,
+            (ends[c], packed[c]), eigen, query_grads, shards[c], places[c], near, mapping, scores,
             unit, tile, begins[c], widths[c],
         )
     if direct:

time: 111 us -> 115 us (1.036)
  waiting for transfers between devices: 20.4 us -> 41.2 us
  starting transfers between devices: 38.7 us -> 21.6 us
  Pallas kernels: 32.3 us -> 34.4 us
    ppermute x0 -> x4, waiting for transfers between devices: none -> 18.5 us  [the longest x1 18.5 us: relay_exchange(): ends = lax.ppermute(far, axis, [(2, 3), (1, 0)])]
    ppermute x4, starting transfers between devices: 19.7 us -> 3.17 us  [scores_of(): scores = scores + lax.ppermute(scores, axis, [(s, s ^ k) for s in range(n)])]
    ppermute x12 -> x9, starting transfers between devices: 19 us -> 10.8 us  [exchange(): got.append(lax.ppermute(payload, axis, [(s, s ^ k) for s in range(n)]))]
    ppermute x0 -> x4, starting transfers between devices: none -> 7.65 us  [the longest x1 3.12 us: relay_exchange(): near = lax.ppermute(mine, axis, [(0, 1), (1, 0), (2, 3), (3, 2)])]
    ppermute x4, waiting for transfers between devices: 6.71 us -> 9.91 us  [scores_of(): scores = scores + lax.ppermute(scores, axis, [(s, s ^ k) for s in range(n)])]
    pallas_call x2, Pallas kernels: 32.3 us -> 34.4 us  [score_part(): pl.pallas_call(kernel, in_specs=[pl.BlockSpec(memory_space=pltpu.SMEM)] *...]
    ppermute x12 -> x9, waiting for transfers between devices: 13.7 us -> 12.8 us  [exchange(): got.append(lax.ppermute(payload, axis, [(s, s ^ k) for s in range(n)]))]
  transfers between devices with their start and end apart: 16 -> 17, of which waited for: 10 -> 9; matrix products, arithmetic and copies ran while one was open for 12% -> 11% of each run, Pallas kernels for 16% -> 15%
where the time goes in v2:
time: 115 us
  waiting for transfers between devices  41.2 us (36%)
  Pallas kernels  34.4 us (30%)
  starting transfers between devices  21.6 us (19%)
  other arithmetic  8.23 us (7%)
  local copies, waits for them, and re-layouts  8.21 us (7%)
    pallas_call x2, Pallas kernels, score_part(): pl.pallas_call(kernel, in_specs=[pl.BlockSpec(memory_space=pltpu.SMEM)] *...  34.4 us
    ppermute x1, waiting for transfers between devices, relay_exchange(): ends = lax.ppermute(far, axis, [(2, 3), (1, 0)])  18.5 us
    ppermute x9, waiting for transfers between devices, exchange(): got.append(lax.ppermute(payload, axis, [(s, s ^ k) for s in range(n)]))  12.8 us
    ppermute x9, starting transfers between devices, exchange(): got.append(lax.ppermute(payload, axis, [(s, s ^ k) for s in range(n)]))  10.8 us
    ppermute x4, waiting for transfers between devices, scores_of(): scores = scores + lax.ppermute(scores, axis, [(s, s ^ k) for s in range(n)])  9.91 us
    ppermute x4, starting transfers between devices, scores_of(): scores = scores + lax.ppermute(scores, axis, [(s, s ^ k) for s in range(n)])  3.17 us
    ppermute x1, starting transfers between devices, relay_exchange(): near = lax.ppermute(mine, axis, [(0, 1), (1, 0), (2, 3), (3, 2)])  3.12 us
    ppermute x1, starting transfers between devices, relay_exchange(): far = lax.ppermute(mine, axis, [(0, 2), (2, 0), (1, 3), (3, 1)])  2.59 us
  transfers between devices with their start and end apart: 17, of which 9 were waited for; matrix products, arithmetic and copies ran while one was open for 11% of the time, Pallas kernels for 15%

profile of v2, /device:TPU:0, one launch (start us, length us, event | category | flops | bytes accessed | tf_op | source)
XLA Modules:
  0.0 114.8 jit_solution(17272909549908797517)
XLA Ops:
  0.7 1.1 fusion.13
  1.8 3.1 %collective-permute-start.6 = (bf16[4,32,1024]{2,1,0:T(8,128)(2,1)S(1)}, bf16[4,32,1024]{2,1,0:T(8,128)(2,1)S(1)}, u32[]{:S(2)}, u32[]{:S(2)}) collective-permute-start(bf16[4,32,1024]{2,1,0:T(8,128)(2,1)S(1)} %get-tuple-element.13.rest_0_), channel_id=1, source_target_pairs={{0,4},{4,0},{8,12},{12,8},{1,5},{5,1},{9,13},{13,9},{2,6},{6,2},{1... | collective-permute-start | bytes 786440 | tf_op jit(solution)/shard_map/ppermute | solution.py:223
  4.9 2.6 %collective-permute-start.7 = (bf16[4,32,1024]{2,1,0:T(8,128)(2,1)S(1)}, bf16[4,32,1024]{2,1,0:T(8,128)(2,1)S(1)}, u32[]{:S(2)}, u32[]{:S(2)}) collective-permute-start(bf16[4,32,1024]{2,1,0:T(8,128)(2,1)S(1)} %get-tuple-element.13.rest_0_), channel_id=1, source_target_pairs={{0,8},{8,0},{4,12},{12,4},{1,9},{9,1},{5,13},{13,5},{2,10},{10,2},... | collective-permute-start | bytes 786440 | tf_op jit(solution)/shard_map/ppermute | solution.py:222
  7.5 0.9 constant_dynamic-slice_fusion.7
  8.4 0.9 pad_maximum_fusion.5
  9.3 1.9 %collective-permute-start.1 = (bf16[2,15360]{1,0:T(2,128)(2,1)S(1)}, bf16[2,15360]{1,0:T(2,128)(2,1)S(1)}, u32[]{:S(2)}, u32[]{:S(2)}) collective-permute-start(bf16[2,15360]{1,0:T(2,128)(2,1)S(1)} %get-tuple-element.26), channel_id=1, source_target_pairs={{0,8},{4,12},{8,0},{12,4},{1,9},{5,13},{9,1},{13,5},{2,10},{6,14},... | collective-permute-start | bytes 184328 | tf_op jit(solution)/shard_map/ppermute | solution.py:217
  11.2 2.5 %collective-permute-start = (bf16[2,15360]{1,0:T(2,128)(2,1)S(1)}, bf16[2,15360]{1,0:T(2,128)(2,1)S(1)}, u32[]{:S(2)}, u32[]{:S(2)}) collective-permute-start(bf16[2,15360]{1,0:T(2,128)(2,1)S(1)} %get-tuple-element.25), channel_id=1, source_target_pairs={{0,4},{4,0},{8,12},{12,8},{1,5},{5,1},{9,13},{13,9},{2,6},{6,2},{1... | collective-permute-start | bytes 184328 | tf_op jit(solution)/shard_map/ppermute | solution.py:217
  13.7 0.6 iota_xor_fusion.place_ref
  14.3 0.2 iota_compare_fusion.1
  15.4 0.2 select_reduce_fusion.5
  15.7 0.7 fusion.2.map_ref
  16.4 0.7 stack.35.place_ref
  17.1 4.4 %collective-permute-done.2 = bf16[2,15360]{1,0:T(2,128)(2,1)S(1)} collective-permute-done((bf16[2,15360]{1,0:T(2,128)(2,1)S(1)}, bf16[2,15360]{1,0:T(2,128)(2,1)S(1)}, u32[]{:S(2)}, u32[]{:S(2)}) %collective-permute-start.2) | collective-permute-done | bytes 61472 | tf_op jit(solution)/shard_map/ppermute | solution.py:217
  21.5 3.0 %collective-permute-done.1 = bf16[2,15360]{1,0:T(2,128)(2,1)S(1)} collective-permute-done((bf16[2,15360]{1,0:T(2,128)(2,1)S(1)}, bf16[2,15360]{1,0:T(2,128)(2,1)S(1)}, u32[]{:S(2)}, u32[]{:S(2)}) %collective-permute-start.1) | collective-permute-done | bytes 61472 | tf_op jit(solution)/shard_map/ppermute | solution.py:217
  24.5 0.3 pad_maximum_fusion.1
  24.8 1.0 dynamic-slice_compare_fusion
  26.4 0.2 add.217
  26.8 0.2 gt.82
  26.9 0.3 gt.83
  27.4 0.3 add.214
  27.7 0.3 fusion
  28.0 0.8 convert_reduce_fusion
  28.8 0.9 select_reduce_fusion
  29.8 1.6 %collective-permute-start.4 = (bf16[8,9216]{1,0:T(8,128)(2,1)S(1)}, bf16[8,9216]{1,0:T(8,128)(2,1)S(1)}, u32[]{:S(2)}, u32[]{:S(2)}) collective-permute-start(bf16[8,9216]{1,0:T(8,128)(2,1)S(1)} %get-tuple-element.19), channel_id=1, source_target_pairs={{0,2},{1,3},{2,0},{3,1},{4,6},{5,7},{6,4},{7,5},{8,10},{9,11},{10,... | collective-permute-start | bytes 442376 | tf_op jit(solution)/shard_map/ppermute | solution.py:217
  31.4 0.3 collective-permute-start.3
  31.7 0.6 fusion.14
  32.3 0.7 slice_reduce_fusion
  33.0 2.9 %collective-permute-done.5 = bf16[8,9216]{1,0:T(8,128)(2,1)S(1)} collective-permute-done((bf16[8,9216]{1,0:T(8,128)(2,1)S(1)}, bf16[8,9216]{1,0:T(8,128)(2,1)S(1)}, u32[]{:S(2)}, u32[]{:S(2)}) %collective-permute-start.5) | collective-permute-done | bytes 147488 | tf_op jit(solution)/shard_map/ppermute | solution.py:217
  35.9 0.7 collective-permute-start.8
  36.6 2.5 %collective-permute-done.4 = bf16[8,9216]{1,0:T(8,128)(2,1)S(1)} collective-permute-done((bf16[8,9216]{1,0:T(8,128)(2,1)S(1)}, bf16[8,9216]{1,0:T(8,128)(2,1)S(1)}, u32[]{:S(2)}, u32[]{:S(2)}) %collective-permute-start.4) | collective-permute-done | bytes 147488 | tf_op jit(solution)/shard_map/ppermute | solution.py:217
  39.1 0.3 collective-permute-start.10
  39.4 2.7 %collective-permute-start.11 = (bf16[4,32,1024]{2,1,0:T(8,128)(2,1)S(1)}, bf16[4,32,1024]{2,1,0:T(8,128)(2,1)S(1)}, u32[]{:S(2)}, u32[]{:S(2)}) collective-permute-start(bf16[4,32,1024]{2,1,0:T(8,128)(2,1)S(1)} %get-tuple-element.12.rest_1_), channel_id=1, source_target_pairs={{0,8},{4,12},{8,0},{12,4},{1,9},{5,13},{9,1},{13,5},{2,10},{6,14},... | collective-permute-start | bytes 786440 | tf_op jit(solution)/shard_map/ppermute | solution.py:217
  42.0 1.5 %collective-permute-start.12 = (bf16[4,32,1024]{2,1,0:T(8,128)(2,1)S(1)}, bf16[4,32,1024]{2,1,0:T(8,128)(2,1)S(1)}, u32[]{:S(2)}, u32[]{:S(2)}) collective-permute-start(bf16[4,32,1024]{2,1,0:T(8,128)(2,1)S(1)} %get-tuple-element.12.rest_1_), channel_id=1, source_target_pairs={{0,12},{4,8},{8,4},{12,0},{1,13},{5,9},{9,5},{13,1},{2,14},{6,10},... | collective-permute-start | bytes 786440 | tf_op jit(solution)/shard_map/ppermute | solution.py:217
  43.6 1.3 %collective-permute-start.9 = (bf16[4,32,1024]{2,1,0:T(8,128)(2,1)S(1)}, bf16[4,32,1024]{2,1,0:T(8,128)(2,1)S(1)}, u32[]{:S(2)}, u32[]{:S(2)}) collective-permute-start(bf16[4,32,1024]{2,1,0:T(8,128)(2,1)S(1)} %collective-permute-done.7.rest_2_), channel_id=1, source_target_pairs={{8,12},{4,0},{9,13},{5,1},{10,14},{6,2},{11,15},{7,3},{24,28},{20,... | collective-permute-start | bytes 786440 | tf_op jit(solution)/shard_map/ppermute | solution.py:225
  44.8 0.9 pad_maximum_fusion.near_ref
  45.7 18.5 %collective-permute-done.9.rest_4_ = bf16[4,32,1024]{2,1,0:T(8,128)(2,1)S(1)} collective-permute-done((bf16[4,32,1024]{2,1,0:T(8,128)(2,1)S(1)}, bf16[4,32,1024]{2,1,0:T(8,128)(2,1)S(1)}, u32[]{:S(2)}, u32[]{:S(2)}) %collective-permute-start.9) | collective-permute-done | bytes 262176 | tf_op jit(solution)/shard_map/ppermute | solution.py:225
  64.2 0.7 copy-done.8
  64.9 17.4 %shard_map.104.rest_0_ = f32[4,128]{1,0:T(4,128)} custom-call(s32[5]{0:T(128)} %stack.35.place_ref, s32[14]{0:T(128)} %get-tuple-element.8.end_ref, s32[936]{0:T(1024)} %bitcast.21, bf16[7168,2048]{1,0:T(8,128)(2,1)} %eigen_hbm.3, bf16[4,128,7168]{2,1,0:T(8,128)(2,1)} %queries_hbm.3, bf16[32,9216]{1,0:T(8,128)(2,1)} %pad_maximum_fusion.near_ref, ...), custom_call_target="tpu_custom_call" | custom-call | tf_op jit(solution)/shard_map/pallas_call | solution.py:191
  82.4 0.7 copy-done.4
  83.3 17.0 %shard_map.105 = f32[4,128]{1,0:T(4,128)} custom-call(s32[4]{0:T(128)} %iota_xor_fusion.place_ref, s32[14]{0:T(128)} %get-tuple-element.9.end_ref, s32[936]{0:T(1024)} %bitcast.20, bf16[7168,2048]{1,0:T(8,128)(2,1)} %eigen_hbm.3, bf16[4,128,7168]{2,1,0:T(8,128)(2,1)} %queries_hbm.3, bf16[32,9216]{1,0:T(8,128)(2,1)} %pad_maximum_fusion.near_ref, ...), custom_call_target="tpu_custom_call" | custom-call | tf_op jit(solution)/shard_map/pallas_call | solution.py:191
  100.4 1.4 %collective-permute-done.13 = f32[4,128]{1,0:T(4,128)S(1)} collective-permute-done((f32[4,128]{1,0:T(4,128)}, f32[4,128]{1,0:T(4,128)S(1)}, u32[]{:S(2)}, u32[]{:S(2)}) %collective-permute-start.13) | collective-permute-done | bytes 2080 | tf_op jit(solution)/shard_map/ppermute | solution.py:321
  101.8 0.7 add.234
  102.4 3.6 %collective-permute-done.14 = f32[4,128]{1,0:T(4,128)S(1)} collective-permute-done((f32[4,128]{1,0:T(4,128)S(1)}, f32[4,128]{1,0:T(4,128)S(1)}, u32[]{:S(2)}, u32[]{:S(2)}) %collective-permute-start.14) | collective-permute-done | bytes 2080 | tf_op jit(solution)/shard_map/ppermute | solution.py:321
  106.0 0.6 collective-permute-start.15
  106.6 3.0 %collective-permute-done.15 = f32[4,128]{1,0:T(4,128)S(1)} collective-permute-done((f32[4,128]{1,0:T(4,128)S(1)}, f32[4,128]{1,0:T(4,128)S(1)}, u32[]{:S(2)}, u32[]{:S(2)}) %collective-permute-start.15) | collective-permute-done | bytes 2080 | tf_op jit(solution)/shard_map/ppermute | solution.py:321
  109.6 2.5 %collective-permute-start.16 = (f32[4,128]{1,0:T(4,128)S(1)}, f32[4,128]{1,0:T(4,128)S(1)}, u32[]{:S(2)}, u32[]{:S(2)}) collective-permute-start(f32[4,128]{1,0:T(4,128)S(1)} %add.236), channel_id=1, source_target_pairs={{0,8},{4,12},{8,0},{12,4},{1,9},{5,13},{9,1},{13,5},{2,10},{6,14},... | collective-permute-start | bytes 6152 | tf_op jit(solution)/shard_map/ppermute | solution.py:321
  112.1 2.0 %collective-permute-done.16 = f32[4,128]{1,0:T(4,128)S(1)} collective-permute-done((f32[4,128]{1,0:T(4,128)S(1)}, f32[4,128]{1,0:T(4,128)S(1)}, u32[]{:S(2)}, u32[]{:S(2)}) %collective-permute-start.16) | collective-permute-done | bytes 2080 | tf_op jit(solution)/shard_map/ppermute | solution.py:321
  114.1 0.6 slice.46
  (71 shorter events, 2.4 us)
Async XLA Ops:
  0.6 23.9 %copy-start.9 = (bf16[2,8192]{1,0:T(2,128)(2,1)S(1)}, bf16[2,8192]{1,0:T(2,128)(2,1)}, u32[]{:S(2)}) copy-start(bf16[2,8192]{1,0:T(2,128)(2,1)} %param.9) | copy-start | bytes 98308
  0.6 14.7 %copy-start.11 = (s32[32]{0:T(128)S(1)}, s32[32]{0:T(128)}, u32[]{:S(2)}) copy-start(s32[32]{0:T(128)} %param.15) | copy-start | bytes 388
  0.7 14.9 %copy-start.12 = (s32[32]{0:T(128)S(1)}, s32[32]{0:T(128)}, u32[]{:S(2)}) copy-start(s32[32]{0:T(128)} %param.16) | copy-start | bytes 388
  1.7 34.1 %copy-start.1 = (bf16[4,32,1024]{2,1,0:T(8,128)(2,1)}, bf16[4,32,1024]{2,1,0:T(8,128)(2,1)S(1)}, u32[]{:S(2)}) copy-start(bf16[4,32,1024]{2,1,0:T(8,128)(2,1)S(1)} %get-tuple-element.13.rest_0_) | copy-start | bytes 786436
  1.8 40.3 %copy-start = (bf16[4,32,1024]{2,1,0:T(8,128)(2,1)}, bf16[4,32,1024]{2,1,0:T(8,128)(2,1)S(1)}, u32[]{:S(2)}) copy-start(bf16[4,32,1024]{2,1,0:T(8,128)(2,1)S(1)} %get-tuple-element.12.rest_1_) | copy-start | bytes 786436
  1.8 40.3 %collective-permute-start.6 = (bf16[4,32,1024]{2,1,0:T(8,128)(2,1)S(1)}, bf16[4,32,1024]{2,1,0:T(8,128)(2,1)S(1)}, u32[]{:S(2)}, u32[]{:S(2)}) collective-permute-start(bf16[4,32,1024]{2,1,0:T(8,128)(2,1)S(1)} %get-tuple-element.13.rest_0_), channel_id=1, source_target_pairs={{0,4},{4,0},{8,12},{12,8},{1,5},{5,1},{9,13},{13,9},{2,6},{6,2},{1... | collective-permute-start | bytes 786440 | tf_op jit(solution)/shard_map/ppermute | solution.py:223
  4.9 38.7 %collective-permute-start.7 = (bf16[4,32,1024]{2,1,0:T(8,128)(2,1)S(1)}, bf16[4,32,1024]{2,1,0:T(8,128)(2,1)S(1)}, u32[]{:S(2)}, u32[]{:S(2)}) collective-permute-start(bf16[4,32,1024]{2,1,0:T(8,128)(2,1)S(1)} %get-tuple-element.13.rest_0_), channel_id=1, source_target_pairs={{0,8},{8,0},{4,12},{12,4},{1,9},{9,1},{5,13},{13,5},{2,10},{10,2},... | collective-permute-start | bytes 786440 | tf_op jit(solution)/shard_map/ppermute | solution.py:222
  9.2 12.2 %collective-permute-start.2 = (bf16[2,15360]{1,0:T(2,128)(2,1)S(1)}, bf16[2,15360]{1,0:T(2,128)(2,1)S(1)}, u32[]{:S(2)}, u32[]{:S(2)}) collective-permute-start(bf16[2,15360]{1,0:T(2,128)(2,1)S(1)} %get-tuple-element.27), channel_id=1, source_target_pairs={{0,12},{4,8},{8,4},{12,0},{1,13},{5,9},{9,5},{13,1},{2,14},{6,10},... | collective-permute-start | bytes 184328 | tf_op jit(solution)/shard_map/ppermute | solution.py:217
  9.3 15.2 %collective-permute-start.1 = (bf16[2,15360]{1,0:T(2,128)(2,1)S(1)}, bf16[2,15360]{1,0:T(2,128)(2,1)S(1)}, u32[]{:S(2)}, u32[]{:S(2)}) collective-permute-start(bf16[2,15360]{1,0:T(2,128)(2,1)S(1)} %get-tuple-element.26), channel_id=1, source_target_pairs={{0,8},{4,12},{8,0},{12,4},{1,9},{5,13},{9,1},{13,5},{2,10},{6,14},... | collective-permute-start | bytes 184328 | tf_op jit(solution)/shard_map/ppermute | solution.py:217
  11.2 13.3 %collective-permute-start = (bf16[2,15360]{1,0:T(2,128)(2,1)S(1)}, bf16[2,15360]{1,0:T(2,128)(2,1)S(1)}, u32[]{:S(2)}, u32[]{:S(2)}) collective-permute-start(bf16[2,15360]{1,0:T(2,128)(2,1)S(1)} %get-tuple-element.25), channel_id=1, source_target_pairs={{0,4},{4,0},{8,12},{12,8},{1,5},{5,1},{9,13},{13,9},{2,6},{6,2},{1... | collective-permute-start | bytes 184328 | tf_op jit(solution)/shard_map/ppermute | solution.py:217
  29.7 6.2 %collective-permute-start.5 = (bf16[8,9216]{1,0:T(8,128)(2,1)S(1)}, bf16[8,9216]{1,0:T(8,128)(2,1)S(1)}, u32[]{:S(2)}, u32[]{:S(2)}) collective-permute-start(bf16[8,9216]{1,0:T(8,128)(2,1)S(1)} %get-tuple-element.20), channel_id=1, source_target_pairs={{0,3},{1,2},{2,1},{3,0},{4,7},{5,6},{6,5},{7,4},{8,11},{9,10},{10,... | collective-permute-start | bytes 442376 | tf_op jit(solution)/shard_map/ppermute | solution.py:217
  29.8 9.3 %collective-permute-start.4 = (bf16[8,9216]{1,0:T(8,128)(2,1)S(1)}, bf16[8,9216]{1,0:T(8,128)(2,1)S(1)}, u32[]{:S(2)}, u32[]{:S(2)}) collective-permute-start(bf16[8,9216]{1,0:T(8,128)(2,1)S(1)} %get-tuple-element.19), channel_id=1, source_target_pairs={{0,2},{1,3},{2,0},{3,1},{4,6},{5,7},{6,4},{7,5},{8,10},{9,11},{10,... | collective-permute-start | bytes 442376 | tf_op jit(solution)/shard_map/ppermute | solution.py:217
  31.4 8.0 %collective-permute-start.3 = (bf16[8,9216]{1,0:T(8,128)(2,1)S(1)}, bf16[8,9216]{1,0:T(8,128)(2,1)S(1)}, u32[]{:S(2)}, u32[]{:S(2)}) collective-permute-start(bf16[8,9216]{1,0:T(8,128)(2,1)S(1)} %get-tuple-element.18), channel_id=1, source_target_pairs={{0,1},{1,0},{2,3},{3,2},{4,5},{5,4},{6,7},{7,6},{8,9},{9,8},{10,11... | collective-permute-start | bytes 442376 | tf_op jit(solution)/shard_map/ppermute | solution.py:217
  35.9 9.8 %collective-permute-start.8 = (bf16[4,32,1024]{2,1,0:T(8,128)(2,1)S(1)}, bf16[4,32,1024]{2,1,0:T(8,128)(2,1)S(1)}, u32[]{:S(2)}, u32[]{:S(2)}) collective-permute-start(bf16[4,32,1024]{2,1,0:T(8,128)(2,1)S(1)} %get-tuple-element.13.rest_0_), channel_id=1, source_target_pairs={{4,8},{8,4},{5,9},{9,5},{6,10},{10,6},{7,11},{11,7},{20,24},{24,20... | collective-permute-start | bytes 786440 | tf_op jit(solution)/shard_map/ppermute | solution.py:224
  39.1 43.3 %collective-permute-start.10 = (bf16[4,32,1024]{2,1,0:T(8,128)(2,1)S(1)}, bf16[4,32,1024]{2,1,0:T(8,128)(2,1)S(1)}, u32[]{:S(2)}, u32[]{:S(2)}) collective-permute-start(bf16[4,32,1024]{2,1,0:T(8,128)(2,1)S(1)} %get-tuple-element.12.rest_1_), channel_id=1, source_target_pairs={{0,4},{4,0},{8,12},{12,8},{1,5},{5,1},{9,13},{13,9},{2,6},{6,2},{1... | collective-permute-start | bytes 786440 | tf_op jit(solution)/shard_map/ppermute | solution.py:217
  39.4 43.0 %collective-permute-start.11 = (bf16[4,32,1024]{2,1,0:T(8,128)(2,1)S(1)}, bf16[4,32,1024]{2,1,0:T(8,128)(2,1)S(1)}, u32[]{:S(2)}, u32[]{:S(2)}) collective-permute-start(bf16[4,32,1024]{2,1,0:T(8,128)(2,1)S(1)} %get-tuple-element.12.rest_1_), channel_id=1, source_target_pairs={{0,8},{4,12},{8,0},{12,4},{1,9},{5,13},{9,1},{13,5},{2,10},{6,14},... | collective-permute-start | bytes 786440 | tf_op jit(solution)/shard_map/ppermute | solution.py:217
  42.0 22.2 %copy-start.2 = (bf16[4,32,1024]{2,1,0:T(8,128)(2,1)}, bf16[4,32,1024]{2,1,0:T(8,128)(2,1)S(1)}, u32[]{:S(2)}) copy-start(bf16[4,32,1024]{2,1,0:T(8,128)(2,1)S(1)} %collective-permute-done.6.rest_1_) | copy-start | bytes 786436
  42.0 40.3 %collective-permute-start.12 = (bf16[4,32,1024]{2,1,0:T(8,128)(2,1)S(1)}, bf16[4,32,1024]{2,1,0:T(8,128)(2,1)S(1)}, u32[]{:S(2)}, u32[]{:S(2)}) collective-permute-start(bf16[4,32,1024]{2,1,0:T(8,128)(2,1)S(1)} %get-tuple-element.12.rest_1_), channel_id=1, source_target_pairs={{0,12},{4,8},{8,4},{12,0},{1,13},{5,9},{9,5},{13,1},{2,14},{6,10},... | collective-permute-start | bytes 786440 | tf_op jit(solution)/shard_map/ppermute | solution.py:217
  43.6 20.7 %copy-start.3 = (bf16[4,32,1024]{2,1,0:T(8,128)(2,1)}, bf16[4,32,1024]{2,1,0:T(8,128)(2,1)S(1)}, u32[]{:S(2)}) copy-start(bf16[4,32,1024]{2,1,0:T(8,128)(2,1)S(1)} %collective-permute-done.7.rest_2_) | copy-start | bytes 786436
  43.6 20.7 %collective-permute-start.9 = (bf16[4,32,1024]{2,1,0:T(8,128)(2,1)S(1)}, bf16[4,32,1024]{2,1,0:T(8,128)(2,1)S(1)}, u32[]{:S(2)}, u32[]{:S(2)}) collective-permute-start(bf16[4,32,1024]{2,1,0:T(8,128)(2,1)S(1)} %collective-permute-done.7.rest_2_), channel_id=1, source_target_pairs={{8,12},{4,0},{9,13},{5,1},{10,14},{6,2},{11,15},{7,3},{24,28},{20,... | collective-permute-start | bytes 786440 | tf_op jit(solution)/shard_map/ppermute | solution.py:225
  45.7 18.5 %copy-start.6 = (bf16[4,32,1024]{2,1,0:T(8,128)(2,1)}, bf16[4,32,1024]{2,1,0:T(8,128)(2,1)S(1)}, u32[]{:S(2)}) copy-start(bf16[4,32,1024]{2,1,0:T(8,128)(2,1)S(1)} %collective-permute-done.8.rest_3_) | copy-start | bytes 786436
  64.2 0.7 copy-start.8
  82.4 0.7 copy-start.4
  82.4 0.8 copy-start.5
  82.4 0.9 copy-start.7
  100.3 1.4 %collective-permute-start.13 = (f32[4,128]{1,0:T(4,128)}, f32[4,128]{1,0:T(4,128)S(1)}, u32[]{:S(2)}, u32[]{:S(2)}) collective-permute-start(f32[4,128]{1,0:T(4,128)} %shard_map.105), channel_id=1, source_target_pairs={{0,1},{1,0},{2,3},{3,2},{4,5},{5,4},{6,7},{7,6},{8,9},{9,8},{10,11... | collective-permute-start | bytes 6152 | tf_op jit(solution)/shard_map/ppermute | solution.py:321
  102.4 3.6 %collective-permute-start.14 = (f32[4,128]{1,0:T(4,128)S(1)}, f32[4,128]{1,0:T(4,128)S(1)}, u32[]{:S(2)}, u32[]{:S(2)}) collective-permute-start(f32[4,128]{1,0:T(4,128)S(1)} %add.234), channel_id=1, source_target_pairs={{0,2},{1,3},{2,0},{3,1},{4,6},{5,7},{6,4},{7,5},{8,10},{9,11},{10,... | collective-permute-start | bytes 6152 | tf_op jit(solution)/shard_map/ppermute | solution.py:321
  106.0 3.6 %collective-permute-start.15 = (f32[4,128]{1,0:T(4,128)S(1)}, f32[4,128]{1,0:T(4,128)S(1)}, u32[]{:S(2)}, u32[]{:S(2)}) collective-permute-start(f32[4,128]{1,0:T(4,128)S(1)} %add.235), channel_id=1, source_target_pairs={{0,4},{4,0},{8,12},{12,8},{1,5},{5,1},{9,13},{13,9},{2,6},{6,2},{1... | collective-permute-start | bytes 6152 | tf_op jit(solution)/shard_map/ppermute | solution.py:321
  109.6 4.5 %collective-permute-start.16 = (f32[4,128]{1,0:T(4,128)S(1)}, f32[4,128]{1,0:T(4,128)S(1)}, u32[]{:S(2)}, u32[]{:S(2)}) collective-permute-start(f32[4,128]{1,0:T(4,128)S(1)} %add.236), channel_id=1, source_target_pairs={{0,8},{4,12},{8,0},{12,4},{1,9},{5,13},{9,1},{13,5},{2,10},{6,14},... | collective-permute-start | bytes 6152 | tf_op jit(solution)/shard_map/ppermute | solution.py:321
  114.1 0.7 copy-start.10

commit v3 on v2

--- a/solution.py
+++ b/solution.py
@@ -11,9 +11,9 @@
 
 BLOCK = 128
 SEQS = 4
-UNROLL = 24
+UNROLL = 16
 FLIGHT = 4
-FIRST_SHARE = 8
+FIRST_SHARE = 9
 SLOT_BITS = 10
 
 damping = 0.1
@@ -179,6 +179,10 @@
     return ends, packed
 
 
+def in_vmem(x):
+    return pltpu.with_memory_space_constraint(x, pltpu.VMEM)
+
+
 def score_part(lists, eigen, query_grads, shards, places, near, mapping, base, unit, piece, first_col, width):
     queries = query_grads.shape[0]
     rows = eigen.shape[0]
@@ -202,8 +206,8 @@
             *[pltpu.VMEM((2, unit, BLOCK), jnp.bfloat16)] * UNROLL,
         ],
         out_shape=jax.ShapeDtypeStruct((queries, mapping.shape[1]), jnp.float32),
-        compiler_params=pltpu.CompilerParams(vmem_limit_bytes=56 << 20),
-    )(places, *lists, eigen, query_grads, near, mapping, *extra, *shards)
+        compiler_params=pltpu.CompilerParams(vmem_limit_bytes=48 << 20),
+    )(places, *lists, eigen, query_grads, *map(in_vmem, (near, mapping, *extra, *shards)))
 
 
 def is_small_power(n):

time: 115 us -> 108 us (0.939)
  Pallas kernels: 34.4 us -> 30.2 us
  local copies, waits for them, and re-layouts: 8.21 us -> 6.24 us
  other arithmetic: 8.23 us -> 6.27 us
  starting transfers between devices: 21.6 us -> 22.9 us
    pallas_call x2, Pallas kernels: 34.4 us -> 30.2 us  [score_part(): pl.pallas_call(kernel, in_specs=[pl.BlockSpec(memory_space=pltpu.SMEM)] *...]
    unnamed x26 -> x16, local copies, waits for them, and re-layouts: 1.63 us -> 0.04 us
    ppermute x4, waiting for transfers between devices: 9.91 us -> 8.58 us  [scores_of(): scores = scores + lax.ppermute(scores, axis, [(s, s ^ k) for s in range(n)])]
    ppermute x4, starting transfers between devices: 3.17 us -> 4.46 us  [scores_of(): scores = scores + lax.ppermute(scores, axis, [(s, s ^ k) for s in range(n)])]
    ppermute x9, waiting for transfers between devices: 12.8 us -> 14 us  [exchange(): got.append(lax.ppermute(payload, axis, [(s, s ^ k) for s in range(n)]))]
  transfers between devices with their start and end apart: 17 -> 17, of which waited for: 9 -> 9; matrix products, arithmetic and copies ran while one was open for 11% -> 10% of each run, Pallas kernels for 15% -> 15%
where the time goes in v3:
time: 108 us; the launch traced here: 107 us
  waiting for transfers between devices  40.5 us (38%)
  Pallas kernels  30.2 us (28%)
  starting transfers between devices  22.9 us (21%)
  other arithmetic  6.27 us (6%)
  local copies, waits for them, and re-layouts  6.24 us (6%)
  between operations  1.1 us (1%)
    pallas_call x2, Pallas kernels, score_part(): pl.pallas_call(kernel, in_specs=[pl.BlockSpec(memory_space=pltpu.SMEM)] *...  30.2 us
    ppermute x1, waiting for transfers between devices, relay_exchange(): ends = lax.ppermute(far, axis, [(2, 3), (1, 0)])  18 us
    ppermute x9, waiting for transfers between devices, exchange(): got.append(lax.ppermute(payload, axis, [(s, s ^ k) for s in range(n)]))  14 us
    ppermute x9, starting transfers between devices, exchange(): got.append(lax.ppermute(payload, axis, [(s, s ^ k) for s in range(n)]))  10.8 us
    ppermute x4, waiting for transfers between devices, scores_of(): scores = scores + lax.ppermute(scores, axis, [(s, s ^ k) for s in range(n)])  8.58 us
    ppermute x4, starting transfers between devices, scores_of(): scores = scores + lax.ppermute(scores, axis, [(s, s ^ k) for s in range(n)])  4.46 us
    ppermute x1, starting transfers between devices, relay_exchange(): near = lax.ppermute(mine, axis, [(0, 1), (1, 0), (2, 3), (3, 2)])  3.12 us
    ppermute x1, starting transfers between devices, relay_exchange(): far = lax.ppermute(mine, axis, [(0, 2), (2, 0), (1, 3), (3, 1)])  2.59 us
  transfers between devices with their start and end apart: 17, of which 9 were waited for; matrix products, arithmetic and copies ran while one was open for 10% of the time, Pallas kernels for 15%

profile of v3, /device:TPU:0, one launch (start us, length us, event | category | flops | bytes accessed | tf_op | source)
XLA Modules:
  0.0 107.2 jit_solution(8488047903308887947)
XLA Ops:
  0.7 1.0 slice.43.rest_0_
  1.7 3.1 %collective-permute-start.6 = (bf16[4,32,1152]{2,1,0:T(8,128)(2,1)S(1)}, bf16[4,32,1152]{2,1,0:T(8,128)(2,1)S(1)}, u32[]{:S(2)}, u32[]{:S(2)}) collective-permute-start(bf16[4,32,1152]{2,1,0:T(8,128)(2,1)S(1)} %slice.43.rest_0_), channel_id=1, source_target_pairs={{0,4},{4,0},{8,12},{12,8},{1,5},{5,1},{9,13},{13,9},{2,6},{6,2},{1... | collective-permute-start | bytes 884744 | tf_op jit(solution)/shard_map/ppermute | solution.py:227
  4.8 2.6 %collective-permute-start.7 = (bf16[4,32,1152]{2,1,0:T(8,128)(2,1)S(1)}, bf16[4,32,1152]{2,1,0:T(8,128)(2,1)S(1)}, u32[]{:S(2)}, u32[]{:S(2)}) collective-permute-start(bf16[4,32,1152]{2,1,0:T(8,128)(2,1)S(1)} %slice.43.rest_0_), channel_id=1, source_target_pairs={{0,8},{8,0},{4,12},{12,4},{1,9},{9,1},{5,13},{13,5},{2,10},{10,2},... | collective-permute-start | bytes 884744 | tf_op jit(solution)/shard_map/ppermute | solution.py:226
  7.4 0.9 constant_dynamic-slice_fusion.7
  8.3 0.9 pad_maximum_fusion.5
  9.3 1.9 %collective-permute-start.1 = (bf16[2,15360]{1,0:T(2,128)(2,1)S(1)}, bf16[2,15360]{1,0:T(2,128)(2,1)S(1)}, u32[]{:S(2)}, u32[]{:S(2)}) collective-permute-start(bf16[2,15360]{1,0:T(2,128)(2,1)S(1)} %get-tuple-element.26), channel_id=1, source_target_pairs={{0,8},{4,12},{8,0},{12,4},{1,9},{5,13},{9,1},{13,5},{2,10},{6,14},... | collective-permute-start | bytes 184328 | tf_op jit(solution)/shard_map/ppermute | solution.py:221
  11.2 2.5 %collective-permute-start = (bf16[2,15360]{1,0:T(2,128)(2,1)S(1)}, bf16[2,15360]{1,0:T(2,128)(2,1)S(1)}, u32[]{:S(2)}, u32[]{:S(2)}) collective-permute-start(bf16[2,15360]{1,0:T(2,128)(2,1)S(1)} %get-tuple-element.25), channel_id=1, source_target_pairs={{0,4},{4,0},{8,12},{12,8},{1,5},{5,1},{9,13},{13,9},{2,6},{6,2},{1... | collective-permute-start | bytes 184328 | tf_op jit(solution)/shard_map/ppermute | solution.py:221
  13.7 0.4 iota_compare_fusion.1
  14.1 1.0 slice.44.rest_1_
  15.2 0.2 gt.89
  15.6 0.2 or.52
  15.8 0.2 gt.85
  16.1 0.2 select_reduce_fusion.5
  16.3 0.2 select_reduce_fusion.4
  16.7 6.2 %collective-permute-done.2 = bf16[2,15360]{1,0:T(2,128)(2,1)S(1)} collective-permute-done((bf16[2,15360]{1,0:T(2,128)(2,1)S(1)}, bf16[2,15360]{1,0:T(2,128)(2,1)S(1)}, u32[]{:S(2)}, u32[]{:S(2)}) %collective-permute-start.2) | collective-permute-done | bytes 61472 | tf_op jit(solution)/shard_map/ppermute | solution.py:221
  22.8 3.0 %collective-permute-done.1 = bf16[2,15360]{1,0:T(2,128)(2,1)S(1)} collective-permute-done((bf16[2,15360]{1,0:T(2,128)(2,1)S(1)}, bf16[2,15360]{1,0:T(2,128)(2,1)S(1)}, u32[]{:S(2)}, u32[]{:S(2)}) %collective-permute-start.1) | collective-permute-done | bytes 61472 | tf_op jit(solution)/shard_map/ppermute | solution.py:221
  25.8 0.3 pad_maximum_fusion.1
  26.5 0.2 select_reduce_fusion.1
  26.7 0.2 select_reduce_fusion.3
  27.2 0.3 add.217
  27.5 0.2 gt.82
  27.7 0.3 gt.83
  28.1 0.3 add.214
  28.5 0.3 fusion
  28.8 1.2 %convert_reduce_fusion = s32[2,1120]{1,0:T(2,128)S(1)} fusion(pred[2,1120]{1,0:T(4,128)(4,1)S(1)} %get-tuple-element.12, pred[1120,1120]{1,0:T(8,128)(4,1)S(1)} %iota_compare_fusion.1), kind=kLoop, calls=%fused_computation.2 | loop fusion | flops 7524160 | bytes 1265600 | tf_op jit(solution)/shard_map/reduce_sum | solution.py:166
  30.2 1.6 %collective-permute-start.4 = (bf16[8,9216]{1,0:T(8,128)(2,1)S(1)}, bf16[8,9216]{1,0:T(8,128)(2,1)S(1)}, u32[]{:S(2)}, u32[]{:S(2)}) collective-permute-start(bf16[8,9216]{1,0:T(8,128)(2,1)S(1)} %get-tuple-element.19), channel_id=1, source_target_pairs={{0,2},{1,3},{2,0},{3,1},{4,6},{5,7},{6,4},{7,5},{8,10},{9,11},{10,... | collective-permute-start | bytes 442376 | tf_op jit(solution)/shard_map/ppermute | solution.py:221
  31.8 0.3 collective-permute-start.3
  32.1 1.6 %select_reduce_fusion = s32[2,1136]{1,0:T(2,128)S(1)} fusion(s32[2,1120]{1,0:T(2,128)S(1)} %get-tuple-element.13, s32[2,1120]{1,0:T(2,128)S(1)} %broadcast_select_fusion.1), kind=kLoop, calls=%fused_computation | loop fusion | flops 7631648 | bytes 27008 | tf_op jit(solution)/shard_map/reduce_sum | solution.py:169
  33.8 0.2 slice_reduce_fusion
  34.1 2.3 %collective-permute-done.5 = bf16[8,9216]{1,0:T(8,128)(2,1)S(1)} collective-permute-done((bf16[8,9216]{1,0:T(8,128)(2,1)S(1)}, bf16[8,9216]{1,0:T(8,128)(2,1)S(1)}, u32[]{:S(2)}, u32[]{:S(2)}) %collective-permute-start.5) | collective-permute-done | bytes 147488 | tf_op jit(solution)/shard_map/ppermute | solution.py:221
  36.3 0.7 collective-permute-start.8
  37.0 2.5 %collective-permute-done.4 = bf16[8,9216]{1,0:T(8,128)(2,1)S(1)} collective-permute-done((bf16[8,9216]{1,0:T(8,128)(2,1)S(1)}, bf16[8,9216]{1,0:T(8,128)(2,1)S(1)}, u32[]{:S(2)}, u32[]{:S(2)}) %collective-permute-start.4) | collective-permute-done | bytes 147488 | tf_op jit(solution)/shard_map/ppermute | solution.py:221
  39.5 0.3 collective-permute-start.10
  39.8 2.8 %collective-permute-start.11 = (bf16[4,32,896]{2,1,0:T(8,128)(2,1)S(1)}, bf16[4,32,896]{2,1,0:T(8,128)(2,1)S(1)}, u32[]{:S(2)}, u32[]{:S(2)}) collective-permute-start(bf16[4,32,896]{2,1,0:T(8,128)(2,1)S(1)} %slice.44.rest_1_), channel_id=1, source_target_pairs={{0,8},{4,12},{8,0},{12,4},{1,9},{5,13},{9,1},{13,5},{2,10},{6,14},... | collective-permute-start | bytes 688136 | tf_op jit(solution)/shard_map/ppermute | solution.py:221
  42.6 1.4 %collective-permute-start.12 = (bf16[4,32,896]{2,1,0:T(8,128)(2,1)S(1)}, bf16[4,32,896]{2,1,0:T(8,128)(2,1)S(1)}, u32[]{:S(2)}, u32[]{:S(2)}) collective-permute-start(bf16[4,32,896]{2,1,0:T(8,128)(2,1)S(1)} %slice.44.rest_1_), channel_id=1, source_target_pairs={{0,12},{4,8},{8,4},{12,0},{1,13},{5,9},{9,5},{13,1},{2,14},{6,10},... | collective-permute-start | bytes 688136 | tf_op jit(solution)/shard_map/ppermute | solution.py:221
  43.9 1.3 %collective-permute-start.9 = (bf16[4,32,1152]{2,1,0:T(8,128)(2,1)S(1)}, bf16[4,32,1152]{2,1,0:T(8,128)(2,1)S(1)}, u32[]{:S(2)}, u32[]{:S(2)}) collective-permute-start(bf16[4,32,1152]{2,1,0:T(8,128)(2,1)S(1)} %collective-permute-done.7.rest_2_), channel_id=1, source_target_pairs={{8,12},{4,0},{9,13},{5,1},{10,14},{6,2},{11,15},{7,3},{24,28},{20,... | collective-permute-start | bytes 884744 | tf_op jit(solution)/shard_map/ppermute | solution.py:229
  45.3 18.0 %collective-permute-done.9.rest_4_ = bf16[4,32,1152]{2,1,0:T(8,128)(2,1)S(1)} collective-permute-done((bf16[4,32,1152]{2,1,0:T(8,128)(2,1)S(1)}, bf16[4,32,1152]{2,1,0:T(8,128)(2,1)S(1)}, u32[]{:S(2)}, u32[]{:S(2)}) %collective-permute-start.9) | collective-permute-done | bytes 294944 | tf_op jit(solution)/shard_map/ppermute | solution.py:229
  63.3 16.5 %shard_map.104.rest_0_ = f32[4,128]{1,0:T(4,128)S(1)} custom-call(s32[5]{0:T(128)S(1)} %stack.35.place_ref, s32[14]{0:T(128)S(1)} %get-tuple-element.10.end_ref, s32[1136]{0:T(1024)S(1)} %get-tuple-element.8.packed_ref, bf16[7168,2048]{1,0:T(8,128)(2,1)} %eigen_hbm.3, bf16[4,128,7168]{2,1,0:T(8,128)(2,1)} %queries_hbm.3, ...), custom_call_target="tpu_custom_call" | custom-call | tf_op jit(solution)/shard_map/pallas_call | solution.py:195
  79.8 13.6 %shard_map.105 = f32[4,128]{1,0:T(4,128)S(1)} custom-call(s32[4]{0:T(128)S(1)} %iota_xor_fusion.place_ref, s32[14]{0:T(128)S(1)} %get-tuple-element.11.end_ref, s32[1136]{0:T(1024)S(1)} %get-tuple-element.9.packed_ref, bf16[7168,2048]{1,0:T(8,128)(2,1)} %eigen_hbm.3, bf16[4,128,7168]{2,1,0:T(8,128)(2,1)} %queries_hbm.3, ...), custom_call_target="tpu_custom_call" | custom-call | tf_op jit(solution)/shard_map/pallas_call | solution.py:195
  93.5 0.4 collective-permute-start.13
  93.8 0.9 collective-permute-done.13
  94.7 0.2 collective-permute-start.14
  94.9 3.4 %collective-permute-done.14 = f32[4,128]{1,0:T(4,128)S(1)} collective-permute-done((f32[4,128]{1,0:T(4,128)S(1)}, f32[4,128]{1,0:T(4,128)S(1)}, u32[]{:S(2)}, u32[]{:S(2)}) %collective-permute-start.14) | collective-permute-done | bytes 2080 | tf_op jit(solution)/shard_map/ppermute | solution.py:325
  98.3 0.8 collective-permute-start.15
  99.1 2.8 %collective-permute-done.15 = f32[4,128]{1,0:T(4,128)S(1)} collective-permute-done((f32[4,128]{1,0:T(4,128)S(1)}, f32[4,128]{1,0:T(4,128)S(1)}, u32[]{:S(2)}, u32[]{:S(2)}) %collective-permute-start.15) | collective-permute-done | bytes 2080 | tf_op jit(solution)/shard_map/ppermute | solution.py:325
  101.9 3.1 %collective-permute-start.16 = (f32[4,128]{1,0:T(4,128)S(1)}, f32[4,128]{1,0:T(4,128)S(1)}, u32[]{:S(2)}, u32[]{:S(2)}) collective-permute-start(f32[4,128]{1,0:T(4,128)S(1)} %add.236), channel_id=1, source_target_pairs={{0,8},{4,12},{8,0},{12,4},{1,9},{5,13},{9,1},{13,5},{2,10},{6,14},... | collective-permute-start | bytes 6152 | tf_op jit(solution)/shard_map/ppermute | solution.py:325
  105.0 1.6 %collective-permute-done.16 = f32[4,128]{1,0:T(4,128)S(1)} collective-permute-done((f32[4,128]{1,0:T(4,128)S(1)}, f32[4,128]{1,0:T(4,128)S(1)}, u32[]{:S(2)}, u32[]{:S(2)}) %collective-permute-start.16) | collective-permute-done | bytes 2080 | tf_op jit(solution)/shard_map/ppermute | solution.py:325
  106.5 0.6 slice.46
  (64 shorter events, 2.0 us)
Async XLA Ops:
  0.6 14.5 %copy-start.7 = (s32[2]{0:T(128)S(1)}, s32[2]{0:T(128)}, u32[]{:S(2)}) copy-start(s32[2]{0:T(128)} %constant.158.clone) | copy-start | bytes 28
  0.6 25.2 %copy-start.1 = (bf16[2,8192]{1,0:T(2,128)(2,1)S(1)}, bf16[2,8192]{1,0:T(2,128)(2,1)}, u32[]{:S(2)}) copy-start(bf16[2,8192]{1,0:T(2,128)(2,1)} %param.9) | copy-start | bytes 98308
  0.7 15.5 %copy-start.5 = (s32[32]{0:T(128)S(1)}, s32[32]{0:T(128)}, u32[]{:S(2)}) copy-start(s32[32]{0:T(128)} %param.15) | copy-start | bytes 388
  0.7 15.6 %copy-start.6 = (s32[32]{0:T(128)S(1)}, s32[32]{0:T(128)}, u32[]{:S(2)}) copy-start(s32[32]{0:T(128)} %param.16) | copy-start | bytes 388
  0.7 25.5 %copy-start = (s32[4,224,64]{1,2,0:T(8,128)S(1)}, s32[4,224,64]{1,2,0:T(8,128)}, u32[]{:S(2)}) copy-start(s32[4,224,64]{1,2,0:T(8,128)} %param.14) | copy-start | bytes 688132
  1.7 40.9 %collective-permute-start.6 = (bf16[4,32,1152]{2,1,0:T(8,128)(2,1)S(1)}, bf16[4,32,1152]{2,1,0:T(8,128)(2,1)S(1)}, u32[]{:S(2)}, u32[]{:S(2)}) collective-permute-start(bf16[4,32,1152]{2,1,0:T(8,128)(2,1)S(1)} %slice.43.rest_0_), channel_id=1, source_target_pairs={{0,4},{4,0},{8,12},{12,8},{1,5},{5,1},{9,13},{13,9},{2,6},{6,2},{1... | collective-permute-start | bytes 884744 | tf_op jit(solution)/shard_map/ppermute | solution.py:227
  4.8 39.1 %collective-permute-start.7 = (bf16[4,32,1152]{2,1,0:T(8,128)(2,1)S(1)}, bf16[4,32,1152]{2,1,0:T(8,128)(2,1)S(1)}, u32[]{:S(2)}, u32[]{:S(2)}) collective-permute-start(bf16[4,32,1152]{2,1,0:T(8,128)(2,1)S(1)} %slice.43.rest_0_), channel_id=1, source_target_pairs={{0,8},{8,0},{4,12},{12,4},{1,9},{9,1},{5,13},{13,5},{2,10},{10,2},... | collective-permute-start | bytes 884744 | tf_op jit(solution)/shard_map/ppermute | solution.py:226
  9.2 13.6 %collective-permute-start.2 = (bf16[2,15360]{1,0:T(2,128)(2,1)S(1)}, bf16[2,15360]{1,0:T(2,128)(2,1)S(1)}, u32[]{:S(2)}, u32[]{:S(2)}) collective-permute-start(bf16[2,15360]{1,0:T(2,128)(2,1)S(1)} %get-tuple-element.27), channel_id=1, source_target_pairs={{0,12},{4,8},{8,4},{12,0},{1,13},{5,9},{9,5},{13,1},{2,14},{6,10},... | collective-permute-start | bytes 184328 | tf_op jit(solution)/shard_map/ppermute | solution.py:221
  9.3 16.6 %collective-permute-start.1 = (bf16[2,15360]{1,0:T(2,128)(2,1)S(1)}, bf16[2,15360]{1,0:T(2,128)(2,1)S(1)}, u32[]{:S(2)}, u32[]{:S(2)}) collective-permute-start(bf16[2,15360]{1,0:T(2,128)(2,1)S(1)} %get-tuple-element.26), channel_id=1, source_target_pairs={{0,8},{4,12},{8,0},{12,4},{1,9},{5,13},{9,1},{13,5},{2,10},{6,14},... | collective-permute-start | bytes 184328 | tf_op jit(solution)/shard_map/ppermute | solution.py:221
  11.2 14.7 %collective-permute-start = (bf16[2,15360]{1,0:T(2,128)(2,1)S(1)}, bf16[2,15360]{1,0:T(2,128)(2,1)S(1)}, u32[]{:S(2)}, u32[]{:S(2)}) collective-permute-start(bf16[2,15360]{1,0:T(2,128)(2,1)S(1)} %get-tuple-element.25), channel_id=1, source_target_pairs={{0,4},{4,0},{8,12},{12,8},{1,5},{5,1},{9,13},{13,9},{2,6},{6,2},{1... | collective-permute-start | bytes 184328 | tf_op jit(solution)/shard_map/ppermute | solution.py:221
  13.7 14.7 %copy-start.3 = (s32[2]{0:T(128)S(1)}, s32[2]{0:T(128)}, u32[]{:S(2)}) copy-start(s32[2]{0:T(128)} %constant.163) | copy-start | bytes 28
  26.1 7.5 %copy-start.4 = (s32[2]{0:T(128)S(1)}, s32[2]{0:T(128)}, u32[]{:S(2)}) copy-start(s32[2]{0:T(128)} %constant.165) | copy-start | bytes 28
  30.2 6.2 %collective-permute-start.5 = (bf16[8,9216]{1,0:T(8,128)(2,1)S(1)}, bf16[8,9216]{1,0:T(8,128)(2,1)S(1)}, u32[]{:S(2)}, u32[]{:S(2)}) collective-permute-start(bf16[8,9216]{1,0:T(8,128)(2,1)S(1)} %get-tuple-element.20), channel_id=1, source_target_pairs={{0,3},{1,2},{2,1},{3,0},{4,7},{5,6},{6,5},{7,4},{8,11},{9,10},{10,... | collective-permute-start | bytes 442376 | tf_op jit(solution)/shard_map/ppermute | solution.py:221
  30.2 9.3 %collective-permute-start.4 = (bf16[8,9216]{1,0:T(8,128)(2,1)S(1)}, bf16[8,9216]{1,0:T(8,128)(2,1)S(1)}, u32[]{:S(2)}, u32[]{:S(2)}) collective-permute-start(bf16[8,9216]{1,0:T(8,128)(2,1)S(1)} %get-tuple-element.19), channel_id=1, source_target_pairs={{0,2},{1,3},{2,0},{3,1},{4,6},{5,7},{6,4},{7,5},{8,10},{9,11},{10,... | collective-permute-start | bytes 442376 | tf_op jit(solution)/shard_map/ppermute | solution.py:221
  31.8 8.0 %collective-permute-start.3 = (bf16[8,9216]{1,0:T(8,128)(2,1)S(1)}, bf16[8,9216]{1,0:T(8,128)(2,1)S(1)}, u32[]{:S(2)}, u32[]{:S(2)}) collective-permute-start(bf16[8,9216]{1,0:T(8,128)(2,1)S(1)} %get-tuple-element.18), channel_id=1, source_target_pairs={{0,1},{1,0},{2,3},{3,2},{4,5},{5,4},{6,7},{7,6},{8,9},{9,8},{10,11... | collective-permute-start | bytes 442376 | tf_op jit(solution)/shard_map/ppermute | solution.py:221
  36.3 8.9 %collective-permute-start.8 = (bf16[4,32,1152]{2,1,0:T(8,128)(2,1)S(1)}, bf16[4,32,1152]{2,1,0:T(8,128)(2,1)S(1)}, u32[]{:S(2)}, u32[]{:S(2)}) collective-permute-start(bf16[4,32,1152]{2,1,0:T(8,128)(2,1)S(1)} %slice.43.rest_0_), channel_id=1, source_target_pairs={{4,8},{8,4},{5,9},{9,5},{6,10},{10,6},{7,11},{11,7},{20,24},{24,20... | collective-permute-start | bytes 884744 | tf_op jit(solution)/shard_map/ppermute | solution.py:228
  39.5 40.3 %collective-permute-start.10 = (bf16[4,32,896]{2,1,0:T(8,128)(2,1)S(1)}, bf16[4,32,896]{2,1,0:T(8,128)(2,1)S(1)}, u32[]{:S(2)}, u32[]{:S(2)}) collective-permute-start(bf16[4,32,896]{2,1,0:T(8,128)(2,1)S(1)} %slice.44.rest_1_), channel_id=1, source_target_pairs={{0,4},{4,0},{8,12},{12,8},{1,5},{5,1},{9,13},{13,9},{2,6},{6,2},{1... | collective-permute-start | bytes 688136 | tf_op jit(solution)/shard_map/ppermute | solution.py:221
  39.8 40.0 %collective-permute-start.11 = (bf16[4,32,896]{2,1,0:T(8,128)(2,1)S(1)}, bf16[4,32,896]{2,1,0:T(8,128)(2,1)S(1)}, u32[]{:S(2)}, u32[]{:S(2)}) collective-permute-start(bf16[4,32,896]{2,1,0:T(8,128)(2,1)S(1)} %slice.44.rest_1_), channel_id=1, source_target_pairs={{0,8},{4,12},{8,0},{12,4},{1,9},{5,13},{9,1},{13,5},{2,10},{6,14},... | collective-permute-start | bytes 688136 | tf_op jit(solution)/shard_map/ppermute | solution.py:221
  42.6 37.2 %collective-permute-start.12 = (bf16[4,32,896]{2,1,0:T(8,128)(2,1)S(1)}, bf16[4,32,896]{2,1,0:T(8,128)(2,1)S(1)}, u32[]{:S(2)}, u32[]{:S(2)}) collective-permute-start(bf16[4,32,896]{2,1,0:T(8,128)(2,1)S(1)} %slice.44.rest_1_), channel_id=1, source_target_pairs={{0,12},{4,8},{8,4},{12,0},{1,13},{5,9},{9,5},{13,1},{2,14},{6,10},... | collective-permute-start | bytes 688136 | tf_op jit(solution)/shard_map/ppermute | solution.py:221
  43.9 19.3 %collective-permute-start.9 = (bf16[4,32,1152]{2,1,0:T(8,128)(2,1)S(1)}, bf16[4,32,1152]{2,1,0:T(8,128)(2,1)S(1)}, u32[]{:S(2)}, u32[]{:S(2)}) collective-permute-start(bf16[4,32,1152]{2,1,0:T(8,128)(2,1)S(1)} %collective-permute-done.7.rest_2_), channel_id=1, source_target_pairs={{8,12},{4,0},{9,13},{5,1},{10,14},{6,2},{11,15},{7,3},{24,28},{20,... | collective-permute-start | bytes 884744 | tf_op jit(solution)/shard_map/ppermute | solution.py:229
  93.5 1.2 %collective-permute-start.13 = (f32[4,128]{1,0:T(4,128)S(1)}, f32[4,128]{1,0:T(4,128)S(1)}, u32[]{:S(2)}, u32[]{:S(2)}) collective-permute-start(f32[4,128]{1,0:T(4,128)S(1)} %shard_map.105), channel_id=1, source_target_pairs={{0,1},{1,0},{2,3},{3,2},{4,5},{5,4},{6,7},{7,6},{8,9},{9,8},{10,11... | collective-permute-start | bytes 6152 | tf_op jit(solution)/shard_map/ppermute | solution.py:325
  94.7 3.6 %collective-permute-start.14 = (f32[4,128]{1,0:T(4,128)S(1)}, f32[4,128]{1,0:T(4,128)S(1)}, u32[]{:S(2)}, u32[]{:S(2)}) collective-permute-start(f32[4,128]{1,0:T(4,128)S(1)} %add.234), channel_id=1, source_target_pairs={{0,2},{1,3},{2,0},{3,1},{4,6},{5,7},{6,4},{7,5},{8,10},{9,11},{10,... | collective-permute-start | bytes 6152 | tf_op jit(solution)/shard_map/ppermute | solution.py:325
  98.3 3.6 %collective-permute-start.15 = (f32[4,128]{1,0:T(4,128)S(1)}, f32[4,128]{1,0:T(4,128)S(1)}, u32[]{:S(2)}, u32[]{:S(2)}) collective-permute-start(f32[4,128]{1,0:T(4,128)S(1)} %add.235), channel_id=1, source_target_pairs={{0,4},{4,0},{8,12},{12,8},{1,5},{5,1},{9,13},{13,9},{2,6},{6,2},{1... | collective-permute-start | bytes 6152 | tf_op jit(solution)/shard_map/ppermute | solution.py:325
  101.9 4.6 %collective-permute-start.16 = (f32[4,128]{1,0:T(4,128)S(1)}, f32[4,128]{1,0:T(4,128)S(1)}, u32[]{:S(2)}, u32[]{:S(2)}) collective-permute-start(f32[4,128]{1,0:T(4,128)S(1)} %add.236), channel_id=1, source_target_pairs={{0,8},{4,12},{8,0},{12,4},{1,9},{5,13},{9,1},{13,5},{2,10},{6,14},... | collective-permute-start | bytes 6152 | tf_op jit(solution)/shard_map/ppermute | solution.py:325
  106.5 0.7 copy-start.2
